TPU v7x, 512 devices: a whole 4x4x16 slice. The times are simulated.
512 devices in a mesh: dp: 128 (over y, z, core), mp: 4 (over x).
Axes of the slice: x: 4, y: 4, z: 16, core: 2. Of those that a mesh axis runs over, the one named last changes fastest.
Arguments:
- embeddings: bfloat16 [32768, 768], P('dp'), may hold values from -8192 to 8192
- cluster_ids: int32 [32768], P('dp'), may hold values from 0 to 511, as said below
Outputs:
- scores: float32 [32768], P('dp')
Inputs may be any that keep to these rules, and one draw needn't show every extreme that they name: `cluster_ids`: the owner of cluster c is the index c // 4 of dp. Of the 256 rows of one index of dp, at most 4 lie in the clusters of one owner, and some owner gets exactly 4 rows from every index of dp.
All inputs are finite; a program needn't handle non-finite values.
Results may differ from a plain program's by a relative error of at most 0.0018.
Values may be sent and summed in bfloat16 or wider, within the bound.
A program may use at most 64 MiB of HBM per device.

v0:
```python
import jax
import jax.numpy as jnp
from jax import lax
from jax.sharding import PartitionSpec as P

CPO = 4


def contract_rows(left_rows, right_rows):
    return lax.dot_general(
        left_rows, right_rows, (((0,), (0,)), ((), ())), preferred_element_type=jnp.float32
    )


def normalize_rows(values):
    widened = values.astype(jnp.float32)
    square_sum = jnp.sum(widened * widened, axis=1, keepdims=True)
    inverse_norm = lax.rsqrt(square_sum + 1e-06)
    return (widened * inverse_norm).astype(jnp.bfloat16)


def best_match(queries, query_ids, query_start, key_units, key_ids):
    similarity = lax.dot_general(
        queries, key_units, (((1,), (1,)), ((), ())), preferred_element_type=jnp.float32
    )
    query_pos = query_start + jnp.arange(queries.shape[0], dtype=jnp.int32)
    key_pos = jnp.arange(key_units.shape[0], dtype=jnp.int32)
    same_cluster = (
        (query_ids[:, None] == key_ids[None, :])
        & (query_ids[:, None] >= 0)
        & (query_pos[:, None] != key_pos[None, :])
    )
    return jnp.max(jnp.where(same_cluster, similarity, -1.0), axis=1)


def local(embeddings, cluster_ids):
    row_count, feat_width = embeddings.shape
    dp_count = lax.axis_size("dp")
    mp_count = lax.axis_size("mp")
    mp_index = lax.axis_index("mp")
    pair_cap = 2 * row_count // dp_count
    slot_count = dp_count * pair_cap
    quarter_len = slot_count // mp_count
    identity = jnp.eye(feat_width, dtype=jnp.float32)
    row_share = row_count // mp_count
    own_rows = lax.dynamic_slice_in_dim(embeddings, mp_index * row_share, row_share, 0)
    moments = lax.psum(contract_rows(own_rows, own_rows), ("dp", "mp"))
    chol_factor = jnp.linalg.cholesky(moments / float(row_count * dp_count) + 0.001 * identity)
    whitening = jax.scipy.linalg.solve_triangular(chol_factor, identity, lower=True).astype(
        jnp.bfloat16
    )
    owner_ids = cluster_ids // CPO
    owner_hits = (owner_ids[:, None] == jnp.arange(dp_count, dtype=jnp.int32)[None, :]).astype(
        jnp.int32
    )
    earlier_hits = jnp.cumsum(owner_hits, axis=0) - owner_hits
    row_rank = jnp.sum(earlier_hits * owner_hits, axis=1)
    col_share = feat_width // mp_count
    whiten_part = lax.dynamic_slice_in_dim(whitening, mp_index * col_share, col_share, 0)
    whitened = lax.dot_general(
        embeddings, whiten_part, (((1,), (1,)), ((), ())), preferred_element_type=jnp.float32
    ).astype(jnp.bfloat16)
    slot_index = owner_ids * pair_cap + row_rank
    send_rows = jnp.zeros((slot_count, col_share), jnp.bfloat16).at[slot_index].set(whitened)
    send_ids = jnp.full((slot_count,), -1, jnp.int32).at[slot_index].set(cluster_ids)
    got_rows, got_ids = (
        lax.all_to_all(send_rows, "dp", split_axis=0, concat_axis=0, tiled=True),
        lax.all_to_all(send_ids, "dp", split_axis=0, concat_axis=0, tiled=True),
    )
    key_rows = lax.all_gather(got_rows, "mp", axis=1, tiled=True)
    unit = normalize_rows(key_rows)
    query_start = mp_index * quarter_len
    queries = lax.dynamic_slice_in_dim(unit, query_start, quarter_len, 0)
    query_ids = lax.dynamic_slice_in_dim(got_ids, query_start, quarter_len, 0)
    best_score = best_match(queries, query_ids, query_start, unit, got_ids)
    all_scores = lax.all_gather(best_score, "mp", axis=0, tiled=True)
    returned = lax.all_to_all(all_scores, "dp", split_axis=0, concat_axis=0, tiled=True)
    return returned[slot_index]


def solution(mesh):
    in_specs = (P("dp", None), P("dp"))
    out_specs = P("dp")
    return jax.shard_map(local, mesh=mesh, in_specs=in_specs, out_specs=out_specs, check_vma=False)
```

profile of v0, /device:TPU:1, one launch (start us, length us, event | category | flops | bytes accessed | tf_op | source)
XLA Modules:
  0.0 857.0 jit_solution(18049372178460269238)
XLA Ops:
  7.5 2.0 fusion.53
  10.2 1.4 scatter_custom_fusion
  12.3 20.5 %all-to-all-start = ((s32[128,4,1]{1,2,0:T(1,128)}), s32[128,4,1]{1,2,0:T(1,128)S(1)}, u32[]{:S(2)}, u32[]{:S(2)}) async-start(s32[128,4,1]{1,2,0:T(1,128)} %bitcast.4), calls=%async_computation | async-start | bytes 131072 | tf_op jit(solution)/shard_map/all_to_all | solution.py:68
  33.9 1.6 fusion.11
  35.4 467.5 %all-reduce.3.cloned.1.call-done = f32[768,768]{0,1:T(8,128)} async-done(((f32[768,768]{0,1:T(8,128)}), f32[768,768]{0,1:T(8,128)}) %all-reduce.3.cloned.1.call-update) | async-done | bytes 2359312 | tf_op jit(solution)/shard_map/psum | solution.py:47
  502.9 3.3 select_add_fusion
  506.3 3.7 copy.39
  510.0 2.0 fusion
  512.0 1.4 copy-done.3
  513.3 11.7 %cholesky.164 = f32[128,128]{1,0:T(8,128)S(1)} custom-call(f32[128,128]{1,0:T(8,128)S(1)} %cholesky.421), custom_call_target="Cholesky" | custom-call | tf_op jit(solution)/shard_map/jit(cholesky)/cholesky | solution.py:48
  525.1 9.8 %custom-call.47 = f32[1,128,128]{1,2,0:T(8,128)S(1)} custom-call(f32[1,128,128]{2,1,0:T(8,128)S(1)} %get-tuple-element.46), custom_call_target="InvertDiagBlocksLowerTriangular" | custom-call | tf_op jit(solution)/shard_map/jit(cholesky)/cholesky | solution.py:48
  534.9 1.4 fusion.33
  536.3 1.4 convolution_subtract_fusion.4
  537.7 11.7 %cholesky.187 = f32[128,128]{1,0:T(8,128)S(1)} custom-call(f32[128,128]{1,0:T(8,128)S(1)} %cholesky.425), custom_call_target="Cholesky" | custom-call | tf_op jit(solution)/shard_map/jit(cholesky)/cholesky | solution.py:48
  550.5 10.6 %custom-call.48 = f32[1,128,128]{1,2,0:T(8,128)} custom-call(f32[1,128,128]{2,1,0:T(8,128)S(1)} %get-tuple-element.44), custom_call_target="InvertDiagBlocksLowerTriangular" | custom-call | tf_op jit(solution)/shard_map/jit(cholesky)/cholesky | solution.py:48
  562.5 1.9 convolution_subtract_fusion.5
  564.5 11.7 %cholesky.352 = f32[128,128]{1,0:T(8,128)S(1)} custom-call(f32[128,128]{1,0:T(8,128)S(1)} %cholesky.430), custom_call_target="Cholesky" | custom-call | tf_op jit(solution)/shard_map/jit(cholesky)/cholesky | solution.py:48
  576.4 9.8 %custom-call.49 = f32[1,128,128]{1,2,0:T(8,128)S(1)} custom-call(f32[1,128,128]{2,1,0:T(8,128)S(1)} %get-tuple-element.42), custom_call_target="InvertDiagBlocksLowerTriangular" | custom-call | tf_op jit(solution)/shard_map/jit(cholesky)/cholesky | solution.py:48
  586.6 2.1 convolution_subtract_fusion.6
  588.7 12.1 %cholesky.371 = f32[128,128]{1,0:T(8,128)S(1)} custom-call(f32[128,128]{1,0:T(8,128)S(1)} %cholesky.435), custom_call_target="Cholesky" | custom-call | tf_op jit(solution)/shard_map/jit(cholesky)/cholesky | solution.py:48
  600.9 9.8 %custom-call.50 = f32[1,128,128]{1,2,0:T(8,128)S(1)} custom-call(f32[1,128,128]{2,1,0:T(8,128)S(1)} %get-tuple-element.40), custom_call_target="InvertDiagBlocksLowerTriangular" | custom-call | tf_op jit(solution)/shard_map/jit(cholesky)/cholesky | solution.py:48
  611.1 1.9 convolution_subtract_fusion.7
  613.0 11.7 %cholesky.390 = f32[128,128]{1,0:T(8,128)S(1)} custom-call(f32[128,128]{1,0:T(8,128)S(1)} %cholesky.440), custom_call_target="Cholesky" | custom-call | tf_op jit(solution)/shard_map/jit(cholesky)/cholesky | solution.py:48
  624.8 9.8 %custom-call.51 = f32[1,128,128]{1,2,0:T(8,128)S(1)} custom-call(f32[1,128,128]{2,1,0:T(8,128)S(1)} %get-tuple-element.38), custom_call_target="InvertDiagBlocksLowerTriangular" | custom-call | tf_op jit(solution)/shard_map/jit(cholesky)/cholesky | solution.py:48
  634.9 1.7 convolution_subtract_fusion.8
  636.7 11.7 %cholesky.408 = f32[128,128]{1,0:T(8,128)S(1)} custom-call(f32[128,128]{1,0:T(8,128)S(1)} %convolution_subtract_fusion.8), custom_call_target="Cholesky" | custom-call | tf_op jit(solution)/shard_map/jit(cholesky)/cholesky | solution.py:48
  655.5 1.6 select_select_fusion
  657.1 21.3 %while.1 = (s32[]{:T(128)}, f32[768,768]{0,1:T(8,128)}, s32[6,2]{0,1:T(2,128)S(1)}, f32[6,128,128]{2,1,0:T(8,128)}, s32[]{:T(128)}) while((s32[]{:T(128)}, f32[768,768]{0,1:T(8,128)}, s32[6,2]{0,1:T(2,128)S(1)}, f32[6,128,128]{2,1,0:T(8,128)}, s32[]{:T(128)}) %tuple.34), condition=%wide.while_cond, body=%wide.while_body.sunk | while | flops 2 | bytes 393829 | solution.py:49
  657.7 2.2 dynamic-slice.7
  661.3 2.2 dynamic-slice.7
  664.9 2.2 dynamic-slice.7
  668.4 2.2 dynamic-slice.7
  672.0 2.2 dynamic-slice.7
  675.5 2.1 dynamic-slice.7
  678.4 59.9 %custom-call.52 = f32[6,128,128]{1,2,0:T(8,128)S(1)} custom-call(f32[6,128,128]{2,1,0:T(8,128)} %get-tuple-element.12), custom_call_target="InvertDiagBlocksLowerTriangular" | custom-call | tf_op jit(solution)/shard_map/jit(_solve_triangular)/triangular_solve | solution.py:49
  739.5 1.8 convolution_subtract_fusion.2
  741.9 2.3 convolution_subtract_fusion.3
  744.8 3.0 convolution_subtract_fusion.1
  748.4 3.6 fusion.12
  752.6 4.6 convolution_subtract_fusion
  758.2 1.5 scatter_custom_fusion.1
  760.5 15.3 %all-to-all-start.1 = ((bf16[128,4,192]{2,1,0:T(4,128)(2,1)}), bf16[128,4,192]{2,1,0:T(4,128)(2,1)S(1)}, u32[]{:S(2)}, u32[]{:S(2)}) async-start(bf16[128,4,192]{2,1,0:T(4,128)(2,1)} %all_to_all.27), calls=%async_computation.1 | async-start | bytes 524288 | tf_op jit(solution)/shard_map/all_to_all | solution.py:67
  777.3 20.9 %all-to-all-done.1 = bf16[128,4,192]{2,1,0:T(4,128)(2,1)S(1)} async-done(((bf16[128,4,192]{2,1,0:T(4,128)(2,1)}), bf16[128,4,192]{2,1,0:T(4,128)(2,1)S(1)}, u32[]{:S(2)}, u32[]{:S(2)}) %all-to-all-start.1) | async-done | bytes 196640 | tf_op jit(solution)/shard_map/all_to_all | solution.py:67
  798.5 11.0 %all_gather.6 = bf16[512,768]{0,1:T(8,128)(2,1)S(1)} all-gather(bf16[512,192]{0,1:T(8,128)(2,1)S(1)} %copy.58), channel_id=1, replica_groups=mesh['dp'=128,'mp'=4] {'mp'}, dimensions={1}, use_global_device_ids=true | all-gather | bytes 983040 | tf_op jit(solution)/shard_map/all_gather | solution.py:70
  810.2 8.2 all-gather
  820.3 11.1 %all-to-all-start.2 = ((f32[128,4,1]{1,2,0:T(1,128)}), f32[128,4,1]{1,2,0:T(1,128)S(1)}, u32[]{:S(2)}, u32[]{:S(2)}) async-start(f32[128,4,1]{1,2,0:T(1,128)} %bitcast.24), calls=%async_computation.2 | async-start | bytes 131072 | tf_op jit(solution)/shard_map/all_to_all | solution.py:77
  831.4 15.1 %all-to-all-done.2 = f32[128,4,1]{1,2,0:T(1,128)S(1)} async-done(((f32[128,4,1]{1,2,0:T(1,128)}), f32[128,4,1]{1,2,0:T(1,128)S(1)}, u32[]{:S(2)}, u32[]{:S(2)}) %all-to-all-start.2) | async-done | bytes 2080 | tf_op jit(solution)/shard_map/all_to_all | solution.py:77
  847.4 2.5 gather_fusion
  (120 shorter events, 29.5 us)
Async XLA Ops:
  6.5 1.0 copy-start
  6.5 496.4 %all-reduce.3.cloned.1.call-start = ((), (), s32[]{:S(2)}) async-start(), calls=%async_computation.3 | async-start | bytes 4718592 | tf_op jit(solution)/shard_map/psum | solution.py:47
  7.5 2.0 copy-start.5
  12.3 748.2 %all-to-all-start = ((s32[128,4,1]{1,2,0:T(1,128)}), s32[128,4,1]{1,2,0:T(1,128)S(1)}, u32[]{:S(2)}, u32[]{:S(2)}) async-start(s32[128,4,1]{1,2,0:T(1,128)} %bitcast.4), calls=%async_computation | async-start | bytes 131072 | tf_op jit(solution)/shard_map/all_to_all | solution.py:68
  506.3 3.7 copy-start.1
  511.9 1.4 copy-start.3
  561.0 1.1 copy-start.4
  678.4 63.5 %copy-start.2 = (f32[768,768]{0,1:T(8,128)S(1)}, f32[768,768]{0,1:T(8,128)}, u32[]{:S(2)}) copy-start(f32[768,768]{0,1:T(8,128)} %fusion.11) | copy-start | bytes 7077892
  760.5 37.7 %all-to-all-start.1 = ((bf16[128,4,192]{2,1,0:T(4,128)(2,1)}), bf16[128,4,192]{2,1,0:T(4,128)(2,1)S(1)}, u32[]{:S(2)}, u32[]{:S(2)}) async-start(bf16[128,4,192]{2,1,0:T(4,128)(2,1)} %all_to_all.27), calls=%async_computation.1 | async-start | bytes 524288 | tf_op jit(solution)/shard_map/all_to_all | solution.py:67
  820.3 26.2 %all-to-all-start.2 = ((f32[128,4,1]{1,2,0:T(1,128)}), f32[128,4,1]{1,2,0:T(1,128)S(1)}, u32[]{:S(2)}, u32[]{:S(2)}) async-start(f32[128,4,1]{1,2,0:T(1,128)} %bitcast.24), calls=%async_computation.2 | async-start | bytes 131072 | tf_op jit(solution)/shard_map/all_to_all | solution.py:77
Sparse Core Ops, SparseCore 0:
  12.6 490.2 all-reduce.2
where the time goes:
time: 862 us; the launch traced here: 857 us
  waiting for transfers between devices  503 us (58%)
  other arithmetic  197 us (23%)
  starting transfers between devices  47 us (5%)
  local copies, waits for them, and re-layouts  39.3 us (5%)
  matrix products  33.7 us (4%)
  blocking collectives  19.1 us (2%)
  between operations  17.9 us (2%)
    psum x1, waiting for transfers between devices, local(): moments = lax.psum(contract_rows(own_rows, own_rows), ('dp', 'mp'))  468 us
    another operation x22, other arithmetic, local(): jnp.linalg.cholesky(moments / float(row_count * dp_count) + 0.001 * ident...  124 us
    another operation x3, other arithmetic, local(): jax.scipy.linalg.solve_triangular(chol_factor, identity, lower=True)  61.5 us
    another operation x33, local copies, waits for them, and re-layouts  21.2 us
    all_to_all x1, waiting for transfers between devices, local(): lax.all_to_all(send_rows, 'dp', split_axis=0, concat_axis=0, tiled=True)  20.9 us
    all_to_all x1, starting transfers between devices, local(): lax.all_to_all(send_ids, 'dp', split_axis=0, concat_axis=0, tiled=True)  20.5 us
    another operation x11, matrix products, local(): jax.scipy.linalg.solve_triangular(chol_factor, identity, lower=True)  19.2 us
  transfers between devices with their start and end apart: 4, of which 3 were waited for; matrix products, arithmetic and copies ran while one was open for 30% of the time, Pallas kernels for 0%

commit v1 on v0

v1 whole, which is shorter than its diff:
```python
import functools

import jax
import jax.numpy as jnp
from jax import lax
from jax.experimental import pallas as pl
from jax.experimental.pallas import tpu as pltpu
from jax.sharding import PartitionSpec as P

CPO = 4
NX, NC, NY, NZ = 4, 2, 4, 16
BLK = 128
NB = 6
D = NB * BLK
MESH = pl.DeviceIdType.MESH
HIGH = lax.Precision.HIGHEST


def moments_kernel(x_ref, out_ref, part, got_c, half, got_y, quarter, got_z,
                   c_send, c_recv, y_send, y_recv, z_send, z_recv,
                   gz_send, gz_recv, a_send, a_recv, b_send, b_recv,
                   a2_send, a2_recv, b2_send, b2_recv, gc_send, gc_recv):
    m = lax.axis_index("mp")
    d = lax.axis_index("dp")
    c = lax.rem(d, 2)
    z = lax.rem(lax.div(d, 2), NZ)
    y = lax.div(d, 2 * NZ)

    def dev(yy, zz, cc, mm):
        return ((yy * NZ + zz) * 2 + cc, mm)

    sibling = dev(y, z, 1 - c, m)
    y_peers = [lax.rem(y + o, NY) for o in (2, 1, 3)]
    z_peers = [lax.rem(z + o, NZ) for o in (8, 7, 9, 6, 10, 5, 11, 4, 12, 3, 13, 2, 14, 1, 15)]
    x_peers = [lax.rem(m + o, NX) for o in (2, 1, 3)]
    barrier = pltpu.get_barrier_semaphore()
    everyone = ([sibling] + [dev(p, z, c, m) for p in y_peers]
                + [dev(y, p, c, m) for p in z_peers] + [dev(y, z, c, p) for p in x_peers])
    for peer in everyone:
        pl.semaphore_signal(barrier, inc=1, device_id=peer, device_id_type=MESH)

    for i in range(NB):
        j = lax.rem(i + m, NB)
        left = x_ref[:, i * BLK:(i + 1) * BLK]
        right = x_ref[:, pl.ds(pl.multiple_of(j * BLK, BLK), BLK)]
        prod = lax.dot_general(left, right, (((0,), (0,)), ((), ())),
                               preferred_element_type=jnp.float32)
        part[:, :, :, i, :] = prod.reshape(NC, NY, NZ, BLK)
    pl.semaphore_wait(barrier, len(everyone))

    def copy(src, dst, send, recv, device):
        return pltpu.make_async_remote_copy(
            src_ref=src, dst_ref=dst, send_sem=send, recv_sem=recv,
            device_id=device, device_id_type=MESH)

    cc = copy(part.at[1 - c], got_c, c_send, c_recv, sibling)
    cc.start()
    cc.wait_recv()
    half[...] = part[c] + got_c[...]
    sent_y = []
    for p in y_peers:
        cp = copy(half.at[p], got_y.at[y], y_send.at[p], y_recv.at[y], dev(p, z, c, m))
        cp.start()
        sent_y.append(cp)
    total = half[y]
    for p in y_peers:
        copy(half.at[p], got_y.at[p], y_send.at[p], y_recv.at[p], dev(p, z, c, m)).wait_recv()
        total = total + got_y[p]
    quarter[...] = total
    sent_z = []
    for p in z_peers:
        cp = copy(quarter.at[p], got_z.at[z], z_send.at[p], z_recv.at[z], dev(y, p, c, m))
        cp.start()
        sent_z.append(cp)
    row = quarter[z]
    for p in reversed(z_peers):
        copy(quarter.at[p], got_z.at[p], z_send.at[p], z_recv.at[p], dev(y, p, c, m)).wait_recv()
        row = row + got_z[p]
    out_ref[m, c, y, z] = row
    gz = []
    for p in z_peers:
        cp = copy(out_ref.at[m, c, y, z], out_ref.at[m, c, y, z], gz_send.at[p], gz_recv.at[z],
                  dev(y, p, c, m))
        cp.start()
        gz.append(cp)
    for p in reversed(z_peers):
        copy(out_ref.at[m, c, y, p], out_ref.at[m, c, y, p], gz_send.at[p], gz_recv.at[p],
             dev(y, p, c, m)).wait_recv()
    lo, hi = pl.ds(0, NZ // 2), pl.ds(NZ // 2, NZ // 2)
    ga = []
    for p in y_peers:
        cp = copy(out_ref.at[m, c, y, lo], out_ref.at[m, c, y, lo], a_send.at[p], a_recv.at[y],
                  dev(p, z, c, m))
        cp.start()
        ga.append(cp)
    for p in x_peers:
        cp = copy(out_ref.at[m, c, y, hi], out_ref.at[m, c, y, hi], b_send.at[p], b_recv.at[m],
                  dev(y, z, c, p))
        cp.start()
        ga.append(cp)
    for p in y_peers:
        copy(out_ref.at[m, c, p, lo], out_ref.at[m, c, p, lo], a_send.at[p], a_recv.at[p],
             dev(p, z, c, m)).wait_recv()
    for p in x_peers:
        cp = copy(out_ref.at[m, c, :, lo], out_ref.at[m, c, :, lo], a2_send.at[p], a2_recv.at[m],
                  dev(y, z, c, p))
        cp.start()
        ga.append(cp)
    for p in x_peers:
        copy(out_ref.at[p, c, y, hi], out_ref.at[p, c, y, hi], b_send.at[p], b_recv.at[p],
             dev(y, z, c, p)).wait_recv()
    for p in y_peers:
        cp = copy(out_ref.at[:, c, y, hi], out_ref.at[:, c, y, hi], b2_send.at[p], b2_recv.at[y],
                  dev(p, z, c, m))
        cp.start()
        ga.append(cp)
    for p in x_peers:
        copy(out_ref.at[p, c, :, lo], out_ref.at[p, c, :, lo], a2_send.at[p], a2_recv.at[p],
             dev(y, z, c, p)).wait_recv()
    for p in y_peers:
        copy(out_ref.at[:, c, p, hi], out_ref.at[:, c, p, hi], b2_send.at[p], b2_recv.at[p],
             dev(p, z, c, m)).wait_recv()
    gc = copy(out_ref.at[:, c], out_ref.at[:, c], gc_send, gc_recv, sibling)
    gc.start()
    copy(out_ref.at[:, 1 - c], out_ref.at[:, 1 - c], gc_send, gc_recv, sibling).wait_recv()
    cc.wait_send()
    for cp in sent_y + sent_z + gz + ga:
        cp.wait_send()
    gc.wait_send()


def summed_moments(x):
    f32 = jnp.float32
    dma = pltpu.SemaphoreType.DMA
    scratch = [
        pltpu.VMEM((NC, NY, NZ, NB, BLK), f32),
        pltpu.VMEM((NY, NZ, NB, BLK), f32),
        pltpu.VMEM((NY, NZ, NB, BLK), f32),
        pltpu.VMEM((NY, NZ, NB, BLK), f32),
        pltpu.VMEM((NZ, NB, BLK), f32),
        pltpu.VMEM((NZ, NB, BLK), f32),
        dma, dma, dma((NY,)), dma((NY,)), dma((NZ,)), dma((NZ,)),
        dma((NZ,)), dma((NZ,)), dma((NY,)), dma((NY,)), dma((NX,)), dma((NX,)),
        dma((NX,)), dma((NX,)), dma((NY,)), dma((NY,)), dma, dma,
    ]
    return pl.pallas_call(
        moments_kernel,
        out_shape=jax.ShapeDtypeStruct((NX, NC, NY, NZ, NB, BLK), f32),
        in_specs=[pl.BlockSpec(memory_space=pltpu.VMEM)],
        out_specs=pl.BlockSpec(memory_space=pltpu.VMEM),
        scratch_shapes=scratch,
        name="moments",
        compiler_params=pltpu.CompilerParams(collective_id=0, has_side_effects=True),
    )(x)


def lower_inverse(block):
    lane = lax.broadcasted_iota(jnp.int32, (8, BLK), 1)
    sub = lax.broadcasted_iota(jnp.int32, (8, BLK), 0)
    groups = BLK // 8
    wide = (8, BLK)
    scales = []
    for t in range(groups):
        own = block[t]
        base = 8 * t
        cols = [jnp.broadcast_to(own[:, base + q:base + q + 1], wide) for q in range(8)]
        piv = [[None] * 8 for _ in range(8)]
        for q in range(8):
            for r in range(q, 8):
                piv[q][r] = jnp.broadcast_to(cols[r][q:q + 1, :], wide)
        mult = [[None] * 8 for _ in range(8)]
        inv = [None] * 8
        scale = None
        for q in range(8):
            inv[q] = 1.0 / piv[q][q]
            for r in range(q + 1, 8):
                mult[q][r] = piv[q][r] * inv[q]
            for r in range(q + 1, 8):
                for s in range(r, 8):
                    piv[r][s] = piv[r][s] - mult[q][r] * piv[q][s]
            root = lax.rsqrt(piv[q][q])
            root = root * (1.5 - 0.5 * piv[q][q] * root * root)
            scale = root if scale is None else jnp.where(sub == q, root, scale)
        scales.append(scale)
        rows = []
        for q in range(8):
            row = jnp.broadcast_to(own[q:q + 1, :], wide)
            row = jnp.where(lane == base + q, inv[q], row * inv[q])
            rows.append(row)
            masked = jnp.where(sub > q, cols[q], 0.0)
            own = jnp.where((lane == base + q) & (sub > q), 0.0, own) - masked * row
            for r in range(q + 1, 8):
                cols[r] = cols[r] - masked * mult[q][r]
        block[t] = own
        for s in range(t + 1, groups):
            cur = block[s]
            coef = [jnp.broadcast_to(cur[:, base + q:base + q + 1], wide) for q in range(8)]
            for q in range(8):
                cur = jnp.where(lane == base + q, 0.0, cur) - coef[q] * rows[q]
                for r in range(q + 1, 8):
                    coef[r] = coef[r] - coef[q] * mult[q][r]
            block[s] = cur
    for t in range(groups):
        diff = lane - sub - 8 * t
        block[t] = scales[t] * jnp.where(diff < 0, block[t], jnp.where(diff == 0, 1.0, 0.0))
    return block


def tdot(a, b):
    return lax.dot_general(a, b, (((0,), (0,)), ((), ())), precision=HIGH,
                           preferred_element_type=jnp.float32)


def score_kernel(row_total, mom_ref, rows_ref, idr_ref, idc_ref, out_ref, work, diag, white):
    scale = 1.0 / row_total
    eye = jnp.where(lax.broadcasted_iota(jnp.int32, (BLK, BLK), 0)
                    == lax.broadcasted_iota(jnp.int32, (BLK, BLK), 1), 0.001, 0.0)

    def at(i, j):
        return (slice(i * BLK, (i + 1) * BLK), slice(j * BLK, (j + 1) * BLK))

    for i in range(NB):
        for g in range(4):
            j = i + g
            if j < NB:
                val = mom_ref[g, :, i, :] * scale
                work[at(i, j)] = val + eye if g == 0 else val
            elif g < 3:
                work[at(j - NB, i)] = (mom_ref[g, :, i, :] * scale).T

    @pl.loop(0, NB)
    def _(k):
        for kk in range(NB):
            @pl.when(k == kk)
            def _():
                diag[...] = work[at(kk, kk)]
        block = lower_inverse([diag[8 * t:8 * t + 8, :] for t in range(BLK // 8)])
        for t in range(BLK // 8):
            diag[8 * t:8 * t + 8, :] = block[t]
        for kk in range(NB):
            @pl.when(k == kk)
            def _():
                rk = slice(kk * BLK, (kk + 1) * BLK)
                inverse = diag[...]
                row = lax.dot_general(inverse, work[rk, :], (((1,), (0,)), ((), ())),
                                      precision=HIGH, preferred_element_type=jnp.float32)
                work[rk, :] = row
                work[at(kk, kk)] = inverse
                for i in range(kk + 1, NB):
                    ri = slice(i * BLK, (i + 1) * BLK)
                    left = work[at(kk, i)]
                    if kk:
                        work[ri, :kk * BLK] = work[ri, :kk * BLK] - tdot(left, work[rk, :kk * BLK])
                    work[at(i, kk)] = -tdot(left, inverse)
                    work[ri, i * BLK:] = work[ri, i * BLK:] - tdot(left, work[rk, i * BLK:])

    for k in range(NB):
        for j in range(NB):
            if j <= k:
                white[at(k, j)] = work[at(k, j)].astype(jnp.bfloat16)
            else:
                white[at(k, j)] = jnp.zeros((BLK, BLK), jnp.bfloat16)
    whitened = lax.dot_general(rows_ref[...], white[...], (((1,), (1,)), ((), ())),
                               preferred_element_type=jnp.float32).astype(jnp.bfloat16)
    widened = whitened.astype(jnp.float32)
    square_sum = jnp.sum(widened * widened, axis=1, keepdims=True)
    unit = (widened * lax.rsqrt(square_sum + 1e-06)).astype(jnp.bfloat16)
    sim = lax.dot_general(unit, unit, (((1,), (1,)), ((), ())), preferred_element_type=jnp.float32)
    slots = sim.shape[0]
    same = (idc_ref[...] == idr_ref[...]) & (idr_ref[...] >= 0)
    other = (lax.broadcasted_iota(jnp.int32, (slots, slots), 0)
             != lax.broadcasted_iota(jnp.int32, (slots, slots), 1))
    out_ref[...] = jnp.max(jnp.where(same & other, sim, -1.0), axis=0, keepdims=True)


def slot_scores(moments, rows, ids, row_total):
    slots = rows.shape[0]
    vm = pl.BlockSpec(memory_space=pltpu.VMEM)
    return pl.pallas_call(
        functools.partial(score_kernel, float(row_total)),
        out_shape=jax.ShapeDtypeStruct((1, slots), jnp.float32),
        in_specs=[vm] * 4,
        out_specs=vm,
        scratch_shapes=[pltpu.VMEM((D, D), jnp.float32), pltpu.VMEM((BLK, BLK), jnp.float32),
                        pltpu.VMEM((D, D), jnp.bfloat16)],
        name="scores",
    )(moments.reshape(NX, NC * NY * NZ, NB, BLK), rows, ids.reshape(1, slots),
      ids.reshape(slots, 1))


def local(embeddings, cluster_ids):
    row_count, feat_width = embeddings.shape
    dp_count = lax.axis_size("dp")
    mp_count = lax.axis_size("mp")
    mp_index = lax.axis_index("mp")
    pair_cap = 2 * row_count // dp_count
    slot_count = dp_count * pair_cap
    moments = summed_moments(embeddings)
    owner_ids = cluster_ids // CPO
    owner_hits = (owner_ids[:, None] == jnp.arange(dp_count, dtype=jnp.int32)[None, :]).astype(
        jnp.int32
    )
    earlier_hits = jnp.cumsum(owner_hits, axis=0) - owner_hits
    row_rank = jnp.sum(earlier_hits * owner_hits, axis=1)
    col_share = feat_width // mp_count
    part = lax.dynamic_slice_in_dim(embeddings, mp_index * col_share, col_share, 1)
    slot_index = owner_ids * pair_cap + row_rank
    send_rows = jnp.zeros((slot_count, col_share), jnp.bfloat16).at[slot_index].set(part)
    send_ids = jnp.full((slot_count,), -1, jnp.int32).at[slot_index].set(cluster_ids)
    got_rows, got_ids = (
        lax.all_to_all(send_rows, "dp", split_axis=0, concat_axis=0, tiled=True),
        lax.all_to_all(send_ids, "dp", split_axis=0, concat_axis=0, tiled=True),
    )
    key_rows = lax.all_gather(got_rows, "mp", axis=1, tiled=True)
    best = slot_scores(moments, key_rows, got_ids, row_count * dp_count)
    returned = lax.all_to_all(best.reshape(slot_count), "dp", split_axis=0, concat_axis=0, tiled=True)
    return returned[slot_index]


def solution(mesh):
    in_specs = (P("dp", None), P("dp"))
    out_specs = P("dp")
    return jax.shard_map(local, mesh=mesh, in_specs=in_specs, out_specs=out_specs, check_vma=False)
```

time: 862 us -> 180 us (0.21)
  waiting for transfers between devices: 503 us -> 27.2 us
  other arithmetic: 197 us -> 5.45 us
  Pallas kernels: 0 us -> 86.4 us
  matrix products: 33.7 us -> 0 us
  local copies, waits for them, and re-layouts: 39.3 us -> 12.6 us
  between operations: 17.9 us -> 0.13 us
  starting transfers between devices: 47 us -> 36.1 us
    psum x1 -> x0, waiting for transfers between devices: 468 us -> none  [local(): moments = lax.psum(contract_rows(own_rows, own_rows), ('dp', 'mp'))]
    another operation x28 -> x3, other arithmetic: 186 us -> 0.25 us  [the longest x22 124 us: local(): jnp.linalg.cholesky(moments / float(row_count * dp_count) + 0.001 * ident...]
    pallas_call x0 -> x2, Pallas kernels: none -> 86.4 us  [the longest x1 49 us: summed_moments(): pl.pallas_call(moments_kernel, out_shape=jax.ShapeDtypeStruct((NX, NC, NY...]
    another operation x21 -> x0, matrix products: 31 us -> none  [the longest x11 19.2 us: local(): jax.scipy.linalg.solve_triangular(chol_factor, identity, lower=True)]
    another operation x54 -> x3, local copies, waits for them, and re-layouts: 23.7 us -> 0.02 us
    all_to_all x1, waiting for transfers between devices: 20.9 us -> 0.01 us  [local(): lax.all_to_all(send_rows, 'dp', split_axis=0, concat_axis=0, tiled=True)]
    all_to_all x1, waiting for transfers between devices: 0.01 us -> 12.2 us  [local(): lax.all_to_all(send_ids, 'dp', split_axis=0, concat_axis=0, tiled=True)]
    all_to_all x1, starting transfers between devices: 15.3 us -> 6.61 us  [local(): lax.all_to_all(send_rows, 'dp', split_axis=0, concat_axis=0, tiled=True)]
  transfers between devices with their start and end apart: 4 -> 3, of which waited for: 3 -> 2; matrix products, arithmetic and copies ran while one was open for 30% -> 3% of each run, Pallas kernels for 0% -> 27%
where the time goes in v1:
time: 180 us
  Pallas kernels  86.4 us (48%)
  starting transfers between devices  36.1 us (20%)
  waiting for transfers between devices  27.2 us (15%)
  local copies, waits for them, and re-layouts  12.6 us (7%)
  blocking collectives  11.7 us (6%)
  other arithmetic  5.45 us (3%)
    pallas_call x1, Pallas kernels, summed_moments(): pl.pallas_call(moments_kernel, out_shape=jax.ShapeDtypeStruct((NX, NC, NY...  49 us
    pallas_call x1, Pallas kernels, slot_scores(): pl.pallas_call(functools.partial(score_kernel, float(row_total)), out_sha...  37.3 us
    all_to_all x1, starting transfers between devices, local(): lax.all_to_all(send_ids, 'dp', split_axis=0, concat_axis=0, tiled=True)  20.6 us
    all_to_all x1, waiting for transfers between devices, local(): lax.all_to_all(best.reshape(slot_count), 'dp', split_axis=0, concat_axis=...  15 us
    all_to_all x1, waiting for transfers between devices, local(): lax.all_to_all(send_ids, 'dp', split_axis=0, concat_axis=0, tiled=True)  12.2 us
    all_gather x1, blocking collectives, local(): key_rows = lax.all_gather(got_rows, 'mp', axis=1, tiled=True)  11.7 us
    all_to_all x1, starting transfers between devices, local(): lax.all_to_all(best.reshape(slot_count), 'dp', split_axis=0, concat_axis=...  8.93 us
    all_to_all x1, starting transfers between devices, local(): lax.all_to_all(send_rows, 'dp', split_axis=0, concat_axis=0, tiled=True)  6.61 us
  transfers between devices with their start and end apart: 3, of which 2 were waited for; matrix products, arithmetic and copies ran while one was open for 3% of the time, Pallas kernels for 27%

profile of v1, /device:TPU:1, one launch (start us, length us, event | category | flops | bytes accessed | tf_op | source)
XLA Modules:
  0.0 179.6 jit_solution(11658029854576187871)
XLA Ops:
  0.0 0.7 fusion.10
  0.7 0.7 and_select_fusion
  1.4 0.1 copy.6
  1.5 0.2 fusion
  1.8 0.2 fusion.2
  2.0 0.7 compare_select_fusion
  2.7 1.6 scatter_custom_fusion.1
  4.2 0.7 all_to_all.25
  5.0 20.6 %all-to-all-start.1 = ((s32[128,4,1]{1,2,0:T(1,128)}), s32[128,4,1]{1,2,0:T(1,128)S(1)}, u32[]{:S(2)}, u32[]{:S(2)}) async-start(s32[128,4,1]{1,2,0:T(1,128)} %bitcast.5), calls=%async_computation.1 | async-start | bytes 131072 | tf_op jit(solution)/shard_map/all_to_all | solution.py:312
  25.5 2.0 %scatter_custom_fusion = bf16[512,192]{1,0:T(8,128)(2,1)S(1)} fusion(s32[256]{0:T(256)S(1)} %compare_select_fusion, bf16[256,768]{1,0:T(8,128)(2,1)} %x_ref.1, s32[]{:T(128)} %constant.28.clone.1, s32[]{:T(128)S(6)} %select_n.15, bf16[]{:T(256)} %constant.12.clone.1), kind=kCustom, calls=%fused_computation.8 | custom fusion | bytes 328708 | tf_op jit(solution)/shard_map/scatter | solution.py:308
  27.5 0.8 all_to_all.22
  28.3 12.2 %all-to-all-done.1 = s32[128,4,1]{1,2,0:T(1,128)S(1)} async-done(((s32[128,4,1]{1,2,0:T(1,128)}), s32[128,4,1]{1,2,0:T(1,128)S(1)}, u32[]{:S(2)}, u32[]{:S(2)}) %all-to-all-start.1) | async-done | bytes 2080 | tf_op jit(solution)/shard_map/all_to_all | solution.py:312
  40.5 6.6 %all-to-all-start = ((bf16[128,4,192]{2,1,0:T(4,128)(2,1)}), bf16[128,4,192]{2,1,0:T(4,128)(2,1)S(1)}, u32[]{:S(2)}, u32[]{:S(2)}) async-start(bf16[128,4,192]{2,1,0:T(4,128)(2,1)} %all_to_all.22), calls=%async_computation | async-start | bytes 524288 | tf_op jit(solution)/shard_map/all_to_all | solution.py:311
  47.1 49.0 %moments.1 = f32[4,2,4,16,6,128]{5,4,3,2,1,0:T(8,128)} custom-call(bf16[256,768]{1,0:T(8,128)(2,1)} %x_ref.1), custom_call_target="tpu_custom_call" | custom-call | tf_op jit(solution)/shard_map/moments/pallas_call | solution.py:146
  96.2 0.8 reshape.66.idc_ref
  97.0 0.5 broadcast.50
  97.5 0.8 reduce.11
  98.3 0.7 reshape.37.idr_ref
  99.0 0.0 all-to-all-done
  99.0 0.2 all_to_all.24
  99.2 0.1 copy.8
  99.3 11.7 %all_gather.3 = bf16[512,768]{0,1:T(8,128)(2,1)S(1)} all-gather(bf16[512,192]{0,1:T(8,128)(2,1)S(1)} %copy.8), channel_id=1, replica_groups=mesh['dp'=128,'mp'=4] {'mp'}, dimensions={1}, use_global_device_ids=true | all-gather | bytes 983040 | tf_op jit(solution)/shard_map/all_gather | solution.py:314
  111.1 1.2 copy.10.rows_ref
  112.3 37.3 %scores.1 = f32[1,512]{1,0:T(1,128)} custom-call(f32[4,128,6,128]{3,2,1,0:T(8,128)} %bitcast.21, bf16[512,768]{1,0:T(8,128)(2,1)} %copy.10.rows_ref, s32[1,512]{1,0:T(1,128)} %reshape.37.idr_ref, s32[512,1]{1,0:T(8,128)} %reshape.66.idc_ref), custom_call_target="tpu_custom_call" | custom-call | tf_op jit(solution)/shard_map/scores/pallas_call | solution.py:279
  149.6 0.5 broadcast.51
  150.1 1.3 reduce.12
  151.5 0.7 all_to_all.27
  152.2 8.9 %all-to-all-start.2 = ((f32[128,4,1]{1,2,0:T(1,128)}), f32[128,4,1]{1,2,0:T(1,128)S(1)}, u32[]{:S(2)}, u32[]{:S(2)}) async-start(f32[128,4,1]{1,2,0:T(1,128)} %bitcast.6), calls=%async_computation.2 | async-start | bytes 131072 | tf_op jit(solution)/shard_map/all_to_all | solution.py:316
  161.1 15.0 %all-to-all-done.2 = f32[128,4,1]{1,2,0:T(1,128)S(1)} async-done(((f32[128,4,1]{1,2,0:T(1,128)}), f32[128,4,1]{1,2,0:T(1,128)S(1)}, u32[]{:S(2)}, u32[]{:S(2)}) %all-to-all-start.2) | async-done | bytes 2080 | tf_op jit(solution)/shard_map/all_to_all | solution.py:316
  176.1 0.8 reduce.13
  176.9 0.1 all_to_all.29
  177.0 2.5 %gather_fusion = f32[256]{0:T(256)} fusion(f32[512]{0:T(512)S(1)} %all_to_all.29, s32[1024]{0:T(1024)S(1)} %pad_clamp_fusion), kind=kCustom, calls=%fused_computation | custom fusion | bytes 3072 | tf_op jit(solution)/shard_map/gather | solution.py:317
  (7 shorter events, 0.1 us)
Async XLA Ops:
  5.0 35.6 %all-to-all-start.1 = ((s32[128,4,1]{1,2,0:T(1,128)}), s32[128,4,1]{1,2,0:T(1,128)S(1)}, u32[]{:S(2)}, u32[]{:S(2)}) async-start(s32[128,4,1]{1,2,0:T(1,128)} %bitcast.5), calls=%async_computation.1 | async-start | bytes 131072 | tf_op jit(solution)/shard_map/all_to_all | solution.py:312
  40.5 58.5 %all-to-all-start = ((bf16[128,4,192]{2,1,0:T(4,128)(2,1)}), bf16[128,4,192]{2,1,0:T(4,128)(2,1)S(1)}, u32[]{:S(2)}, u32[]{:S(2)}) async-start(bf16[128,4,192]{2,1,0:T(4,128)(2,1)} %all_to_all.22), calls=%async_computation | async-start | bytes 524288 | tf_op jit(solution)/shard_map/all_to_all | solution.py:311
  152.2 23.9 %all-to-all-start.2 = ((f32[128,4,1]{1,2,0:T(1,128)}), f32[128,4,1]{1,2,0:T(1,128)S(1)}, u32[]{:S(2)}, u32[]{:S(2)}) async-start(f32[128,4,1]{1,2,0:T(1,128)} %bitcast.6), calls=%async_computation.2 | async-start | bytes 131072 | tf_op jit(solution)/shard_map/all_to_all | solution.py:316

commit v2 on v0

v2 whole, which is shorter than its diff:
```python
import functools

import jax
import jax.numpy as jnp
from jax import lax
from jax.experimental import pallas as pl
from jax.experimental.pallas import tpu as pltpu
from jax.sharding import PartitionSpec as P

CPO = 4
NX, NC, NY, NZ = 4, 2, 4, 16
BLK = 128
NB = 6
D = NB * BLK
N_DP = NC * NY * NZ
PAIR = 4
GATHER_AT = 2
MESH = pl.DeviceIdType.MESH
HIGH = lax.Precision.HIGHEST


def lower_inverse(block):
    lane = lax.broadcasted_iota(jnp.int32, (8, BLK), 1)
    sub = lax.broadcasted_iota(jnp.int32, (8, BLK), 0)
    groups = BLK // 8
    wide = (8, BLK)
    scales = []
    for t in range(groups):
        own = block[t]
        base = 8 * t
        cols = [jnp.broadcast_to(own[:, base + q:base + q + 1], wide) for q in range(8)]
        piv = [[None] * 8 for _ in range(8)]
        for q in range(8):
            for r in range(q, 8):
                piv[q][r] = jnp.broadcast_to(cols[r][q:q + 1, :], wide)
        mult = [[None] * 8 for _ in range(8)]
        inv = [None] * 8
        scale = None
        for q in range(8):
            inv[q] = 1.0 / piv[q][q]
            for r in range(q + 1, 8):
                mult[q][r] = piv[q][r] * inv[q]
            for r in range(q + 1, 8):
                for s in range(r, 8):
                    piv[r][s] = piv[r][s] - mult[q][r] * piv[q][s]
            root = lax.rsqrt(piv[q][q])
            root = root * (1.5 - 0.5 * piv[q][q] * root * root)
            scale = root if scale is None else jnp.where(sub == q, root, scale)
        scales.append(scale)
        rows = []
        for q in range(8):
            row = jnp.broadcast_to(own[q:q + 1, :], wide)
            row = jnp.where(lane == base + q, inv[q], row * inv[q])
            rows.append(row)
            masked = jnp.where(sub > q, cols[q], 0.0)
            own = jnp.where((lane == base + q) & (sub > q), 0.0, own) - masked * row
            for r in range(q + 1, 8):
                cols[r] = cols[r] - masked * mult[q][r]
        block[t] = own
        for s in range(t + 1, groups):
            cur = block[s]
            coef = [jnp.broadcast_to(cur[:, base + q:base + q + 1], wide) for q in range(8)]
            for q in range(8):
                cur = jnp.where(lane == base + q, 0.0, cur) - coef[q] * rows[q]
                for r in range(q + 1, 8):
                    coef[r] = coef[r] - coef[q] * mult[q][r]
            block[s] = cur
    for t in range(groups):
        diff = lane - sub - 8 * t
        block[t] = scales[t] * jnp.where(diff < 0, block[t], jnp.where(diff == 0, 1.0, 0.0))
    return block


def tdot(a, b):
    return lax.dot_general(a, b, (((0,), (0,)), ((), ())), precision=HIGH,
                           preferred_element_type=jnp.float32)


def kernel(row_total, x_ref, ids_ref, out_ref,
           part, got_c, half, got_y, quarter, got_z, mom,
           stage, send_rows, got, work, diag, white, rows, ret, ret_got,
           c_send, c_recv, y_send, y_recv, z_send, z_recv,
           gz_send, gz_recv, a_send, a_recv, b_send, b_recv,
           a2_send, a2_recv, b2_send, b2_recv, gc_send, gc_recv,
           d_send, d_recv, x_send, x_recv, r_send, r_recv):
    f32, bf16 = jnp.float32, jnp.bfloat16
    m = lax.axis_index("mp")
    d = lax.axis_index("dp")
    c = lax.rem(d, 2)
    z = lax.rem(lax.div(d, 2), NZ)
    y = lax.div(d, 2 * NZ)

    def dev(yy, zz, cc, mm):
        return ((yy * NZ + zz) * 2 + cc, mm)

    sibling = dev(y, z, 1 - c, m)
    y_peers = [lax.rem(y + o, NY) for o in (2, 1, 3)]
    z_peers = [lax.rem(z + o, NZ) for o in (8, 7, 9, 6, 10, 5, 11, 4, 12, 3, 13, 2, 14, 1, 15)]
    x_peers = [lax.rem(m + o, NX) for o in (2, 1, 3)]
    barrier = pltpu.get_barrier_semaphore()

    @pl.loop(1, N_DP)
    def _(o):
        pl.semaphore_signal(barrier, inc=1, device_id=(lax.rem(d + o, N_DP), m),
                            device_id_type=MESH)
    for p in x_peers:
        pl.semaphore_signal(barrier, inc=1, device_id=(d, p), device_id_type=MESH)

    for i in range(NB):
        j = lax.rem(i + m, NB)
        left = x_ref[:, i * BLK:(i + 1) * BLK]
        right = x_ref[:, pl.ds(pl.multiple_of(j * BLK, BLK), BLK)]
        prod = lax.dot_general(left, right, (((0,), (0,)), ((), ())),
                               preferred_element_type=f32)
        part[:, :, :, i, :] = prod.reshape(NC, NY, NZ, BLK)

    count = x_ref.shape[0]
    owner = lax.div(ids_ref[...], CPO)
    within = (ids_ref[...] - owner * CPO + 1).astype(f32)
    owner = owner.astype(f32)
    owner_row = jnp.broadcast_to(owner, (count, count))
    first = lax.broadcasted_iota(jnp.int32, (count, count), 0)
    second = lax.broadcasted_iota(jnp.int32, (count, count), 1)
    earlier = (owner_row == owner_row.T) & (first < second)
    rank = jnp.sum(jnp.where(earlier, 1.0, 0.0), axis=0, keepdims=True)
    owner_iota = lax.broadcasted_iota(jnp.int32, (N_DP, count), 0).astype(f32)
    own_hit = owner_iota == owner
    pick = jnp.where(own_hit & (rank == m.astype(f32)), 1.0, 0.0)
    picked = lax.dot_general(pick.astype(bf16), x_ref[...], (((1,), (0,)), ((), ())),
                             preferred_element_type=f32)
    label = jnp.sum(pick * within, axis=1, keepdims=True) - 1.0
    for i in range(NB):
        stage[:, i, :] = picked[:, i * BLK:(i + 1) * BLK]
    stage[:, NB, :] = jnp.broadcast_to(label, (N_DP, BLK))
    stage[:, NB + 1, :] = jnp.zeros((N_DP, BLK), f32)
    send_rows[...] = stage[...].astype(bf16)
    got[m, d] = send_rows[d]
    pl.semaphore_wait(barrier, N_DP - 1 + NX - 1)

    def copy(src, dst, send, recv, device):
        return pltpu.make_async_remote_copy(
            src_ref=src, dst_ref=dst, send_sem=send, recv_sem=recv,
            device_id=device, device_id_type=MESH)

    cc = copy(part.at[1 - c], got_c, c_send, c_recv, sibling)
    cc.start()
    cc.wait_recv()
    half[...] = part[c] + got_c[...]
    sent = []
    for p in y_peers:
        cp = copy(half.at[p], got_y.at[y], y_send.at[p], y_recv.at[y], dev(p, z, c, m))
        cp.start()
        sent.append(cp)
    total = half[y]
    for p in y_peers:
        copy(half.at[p], got_y.at[p], y_send.at[p], y_recv.at[p], dev(p, z, c, m)).wait_recv()
        total = total + got_y[p]
    quarter[...] = total
    for p in z_peers:
        cp = copy(quarter.at[p], got_z.at[z], z_send.at[p], z_recv.at[z], dev(y, p, c, m))
        cp.start()
        sent.append(cp)
    row = quarter[z]
    for p in reversed(z_peers):
        copy(quarter.at[p], got_z.at[p], z_send.at[p], z_recv.at[p], dev(y, p, c, m)).wait_recv()
        row = row + got_z[p]
    mom[m, c, y, z] = row
    for p in z_peers:
        cp = copy(mom.at[m, c, y, z], mom.at[m, c, y, z], gz_send.at[p], gz_recv.at[z],
                  dev(y, p, c, m))
        cp.start()
        sent.append(cp)

    @pl.loop(1, N_DP)
    def _(o):
        p = lax.rem(d + o, N_DP)
        copy(send_rows.at[p], got.at[m, d], d_send, d_recv, (p, m)).start()
    for p in reversed(z_peers):
        copy(mom.at[m, c, y, p], mom.at[m, c, y, p], gz_send.at[p], gz_recv.at[p],
             dev(y, p, c, m)).wait_recv()
    lo, hi = pl.ds(0, NZ // 2), pl.ds(NZ // 2, NZ // 2)
    for p in y_peers:
        cp = copy(mom.at[m, c, y, lo], mom.at[m, c, y, lo], a_send.at[p], a_recv.at[y],
                  dev(p, z, c, m))
        cp.start()
        sent.append(cp)
    for p in x_peers:
        cp = copy(mom.at[m, c, y, hi], mom.at[m, c, y, hi], b_send.at[p], b_recv.at[m],
                  dev(y, z, c, p))
        cp.start()
        sent.append(cp)
    for p in y_peers:
        copy(mom.at[m, c, p, lo], mom.at[m, c, p, lo], a_send.at[p], a_recv.at[p],
             dev(p, z, c, m)).wait_recv()
    for p in x_peers:
        cp = copy(mom.at[m, c, :, lo], mom.at[m, c, :, lo], a2_send.at[p], a2_recv.at[m],
                  dev(y, z, c, p))
        cp.start()
        sent.append(cp)
    for p in x_peers:
        copy(mom.at[p, c, y, hi], mom.at[p, c, y, hi], b_send.at[p], b_recv.at[p],
             dev(y, z, c, p)).wait_recv()
    for p in y_peers:
        cp = copy(mom.at[:, c, y, hi], mom.at[:, c, y, hi], b2_send.at[p], b2_recv.at[y],
                  dev(p, z, c, m))
        cp.start()
        sent.append(cp)
    for p in x_peers:
        copy(mom.at[p, c, :, lo], mom.at[p, c, :, lo], a2_send.at[p], a2_recv.at[p],
             dev(y, z, c, p)).wait_recv()
    for p in y_peers:
        copy(mom.at[:, c, p, hi], mom.at[:, c, p, hi], b2_send.at[p], b2_recv.at[p],
             dev(p, z, c, m)).wait_recv()
    gc = copy(mom.at[:, c], mom.at[:, c], gc_send, gc_recv, sibling)
    gc.start()
    copy(mom.at[:, 1 - c], mom.at[:, 1 - c], gc_send, gc_recv, sibling).wait_recv()
    cc.wait_send()
    for cp in sent:
        cp.wait_send()
    gc.wait_send()

    scale = 1.0 / row_total
    eye = jnp.where(lax.broadcasted_iota(jnp.int32, (BLK, BLK), 0)
                    == lax.broadcasted_iota(jnp.int32, (BLK, BLK), 1), 0.001, 0.0)

    def at(i, j):
        return (slice(i * BLK, (i + 1) * BLK), slice(j * BLK, (j + 1) * BLK))

    def moment_block(g, i):
        return mom[g, :, :, :, i, :].reshape(BLK, BLK) * scale

    for i in range(NB):
        for g in range(4):
            j = i + g
            if j < NB:
                val = moment_block(g, i)
                work[at(i, j)] = val + eye if g == 0 else val
            elif g < 3:
                work[at(j - NB, i)] = moment_block(g, i).T

    @pl.loop(0, NB)
    def _(k):
        for kk in range(NB):
            @pl.when(k == kk)
            def _():
                diag[...] = work[at(kk, kk)]
                if kk == GATHER_AT:
                    copy(send_rows.at[pl.ds(0, N_DP - 1)], got.at[m, pl.ds(0, N_DP - 1)],
                         d_send, d_recv, sibling).wait()
                    for p in x_peers:
                        copy(got.at[m], got.at[m], x_send.at[p], x_recv.at[m],
                             (d, p)).start()
        block = lower_inverse([diag[8 * t:8 * t + 8, :] for t in range(BLK // 8)])
        for t in range(BLK // 8):
            diag[8 * t:8 * t + 8, :] = block[t]
        for kk in range(NB):
            @pl.when(k == kk)
            def _():
                rk = slice(kk * BLK, (kk + 1) * BLK)
                inverse = diag[...]
                line = lax.dot_general(inverse, work[rk, :], (((1,), (0,)), ((), ())),
                                       precision=HIGH, preferred_element_type=f32)
                work[rk, :] = line
                work[at(kk, kk)] = inverse
                for i in range(kk + 1, NB):
                    ri = slice(i * BLK, (i + 1) * BLK)
                    left = work[at(kk, i)]
                    if kk:
                        work[ri, :kk * BLK] = work[ri, :kk * BLK] - tdot(left, work[rk, :kk * BLK])
                    work[at(i, kk)] = -tdot(left, inverse)
                    work[ri, i * BLK:] = work[ri, i * BLK:] - tdot(left, work[rk, i * BLK:])

    for k in range(NB):
        for j in range(NB):
            if j <= k:
                white[at(k, j)] = work[at(k, j)].astype(bf16)
            else:
                white[at(k, j)] = jnp.zeros((BLK, BLK), bf16)

    for p in x_peers:
        copy(got.at[p], got.at[p], x_send.at[p], x_recv.at[p], (d, p)).wait()
    labels = []
    for k in range(PAIR):
        stage[...] = got[k].astype(f32)
        for i in range(NB):
            rows[k * N_DP:(k + 1) * N_DP, i * BLK:(i + 1) * BLK] = stage[:, i, :].astype(bf16)
        labels.append(stage[:, NB, :])
    whitened = lax.dot_general(rows[...], white[...], (((1,), (1,)), ((), ())),
                               preferred_element_type=f32).astype(bf16)
    widened = whitened.astype(f32)
    square_sum = jnp.sum(widened * widened, axis=1, keepdims=True)
    rows[...] = (widened * lax.rsqrt(square_sum + 1e-06)).astype(bf16)
    lane = lax.broadcasted_iota(jnp.int32, (N_DP, N_DP), 1)
    other = lax.broadcasted_iota(jnp.int32, (N_DP, N_DP), 0) != lane
    flipped = [value.T for value in labels]
    reply = jnp.zeros((N_DP, N_DP), f32)
    for a in range(PAIR):
        sim = lax.dot_general(rows[a * N_DP:(a + 1) * N_DP, :], rows[...],
                              (((1,), (1,)), ((), ())), preferred_element_type=f32)
        best = jnp.full((N_DP, N_DP), -1.0, f32)
        for b in range(PAIR):
            same = (labels[a] == flipped[b]) & (labels[a] >= 0.0)
            if a == b:
                same = same & other
            best = jnp.maximum(best, jnp.where(same, sim[:, b * N_DP:(b + 1) * N_DP], -1.0))
        reply = jnp.where(lane == a, jnp.max(best, axis=1, keepdims=True), reply)
    ret[:, 0, :] = reply
    ret_got[d] = ret[d]

    @pl.loop(1, N_DP)
    def _(o):
        p = lax.rem(d + o, N_DP)
        copy(ret.at[p], ret_got.at[d], r_send, r_recv, (p, m)).start()
    copy(ret.at[pl.ds(0, N_DP - 1)], ret_got.at[pl.ds(0, N_DP - 1)], r_send, r_recv,
         sibling).wait()
    table = lax.dot_general(ret_got[:, 0, :], jnp.where(own_hit, 1.0, 0.0),
                            (((0,), (0,)), ((), ())), precision=HIGH, preferred_element_type=f32)
    score = jnp.zeros((1, count), f32)
    for k in range(PAIR):
        score = jnp.where(rank == float(k), table[k:k + 1, :], score)
    out_ref[...] = score


def local(embeddings, cluster_ids):
    row_count, feat_width = embeddings.shape
    dp_count = lax.axis_size("dp")
    f32, bf16 = jnp.float32, jnp.bfloat16
    dma = pltpu.SemaphoreType.DMA
    scratch = [
        pltpu.VMEM((NC, NY, NZ, NB, BLK), f32),
        pltpu.VMEM((NY, NZ, NB, BLK), f32),
        pltpu.VMEM((NY, NZ, NB, BLK), f32),
        pltpu.VMEM((NY, NZ, NB, BLK), f32),
        pltpu.VMEM((NZ, NB, BLK), f32),
        pltpu.VMEM((NZ, NB, BLK), f32),
        pltpu.VMEM((NX, NC, NY, NZ, NB, BLK), f32),
        pltpu.VMEM((N_DP, NB + 2, BLK), f32),
        pltpu.VMEM((N_DP, NB + 2, BLK), bf16),
        pltpu.VMEM((NX, N_DP, NB + 2, BLK), bf16),
        pltpu.VMEM((D, D), f32),
        pltpu.VMEM((BLK, BLK), f32),
        pltpu.VMEM((D, D), bf16),
        pltpu.VMEM((PAIR * N_DP, D), bf16),
        pltpu.VMEM((N_DP, 1, BLK), f32),
        pltpu.VMEM((N_DP, 1, BLK), f32),
        dma, dma, dma((NY,)), dma((NY,)), dma((NZ,)), dma((NZ,)),
        dma((NZ,)), dma((NZ,)), dma((NY,)), dma((NY,)), dma((NX,)), dma((NX,)),
        dma((NX,)), dma((NX,)), dma((NY,)), dma((NY,)), dma, dma,
        dma, dma, dma((NX,)), dma((NX,)), dma, dma,
    ]
    vm = pl.BlockSpec(memory_space=pltpu.VMEM)
    scores = pl.pallas_call(
        functools.partial(kernel, float(row_count * dp_count)),
        out_shape=jax.ShapeDtypeStruct((1, row_count), f32),
        in_specs=[vm, vm],
        out_specs=vm,
        scratch_shapes=scratch,
        name="dedup",
        compiler_params=pltpu.CompilerParams(collective_id=0, has_side_effects=True),
    )(embeddings, cluster_ids.reshape(1, row_count))
    return scores.reshape(row_count)


def solution(mesh):
    in_specs = (P("dp", None), P("dp"))
    out_specs = P("dp")
    return jax.shard_map(local, mesh=mesh, in_specs=in_specs, out_specs=out_specs, check_vma=False)
```

time: 862 us -> 103 us (0.12)
  waiting for transfers between devices: 503 us -> 0 us
  other arithmetic: 197 us -> 0 us
  Pallas kernels: 0 us -> 102 us
  starting transfers between devices: 47 us -> 0 us
  local copies, waits for them, and re-layouts: 39.3 us -> 1.22 us
  matrix products: 33.7 us -> 0 us
  blocking collectives: 19.1 us -> 0 us
  between operations: 17.9 us -> 0.02 us
    psum x1 -> x0, waiting for transfers between devices: 468 us -> none  [local(): moments = lax.psum(contract_rows(own_rows, own_rows), ('dp', 'mp'))]
    another operation x28 -> x0, other arithmetic: 186 us -> none  [the longest x22 124 us: local(): jnp.linalg.cholesky(moments / float(row_count * dp_count) + 0.001 * ident...]
    pallas_call x0 -> x1, Pallas kernels: none -> 102 us  [local(): pl.pallas_call(functools.partial(kernel, float(row_count * dp_count)), ou...]
    all_to_all x3 -> x0, starting transfers between devices: 46.9 us -> none  [the longest x1 20.5 us: local(): lax.all_to_all(send_ids, 'dp', split_axis=0, concat_axis=0, tiled=True)]
    all_to_all x3 -> x0, waiting for transfers between devices: 35.9 us -> none  [the longest x1 20.9 us: local(): lax.all_to_all(send_rows, 'dp', split_axis=0, concat_axis=0, tiled=True)]
    another operation x21 -> x0, matrix products: 31 us -> none  [the longest x11 19.2 us: local(): jax.scipy.linalg.solve_triangular(chol_factor, identity, lower=True)]
    another operation x54 -> x0, local copies, waits for them, and re-layouts: 23.7 us -> none
    all_gather x2 -> x0, blocking collectives: 19.1 us -> none  [the longest x1 11 us: local(): key_rows = lax.all_gather(got_rows, 'mp', axis=1, tiled=True)]
  transfers between devices with their start and end apart: 4 -> 0, of which waited for: 3 -> 0; matrix products, arithmetic and copies ran while one was open for 30% -> 0% of each run, Pallas kernels for 0% -> 0%
where the time goes in v2:
time: 103 us
  Pallas kernels  102 us (99%)
  local copies, waits for them, and re-layouts  1.22 us (1%)
    pallas_call x1, Pallas kernels, local(): pl.pallas_call(functools.partial(kernel, float(row_count * dp_count)), ou...  102 us

profile of v2, /device:TPU:1, one launch (start us, length us, event | category | flops | bytes accessed | tf_op | source)
XLA Modules:
  0.0 102.8 jit_solution(2724255734792824507)
XLA Ops:
  0.0 101.6 %dedup.1 = f32[1,256]{1,0:T(1,128)} custom-call(bf16[256,768]{1,0:T(8,128)(2,1)} %x_ref.1, s32[1,256]{1,0:T(1,128)} %bitcast.3), custom_call_target="tpu_custom_call" | custom-call | tf_op jit(solution)/shard_map/dedup/pallas_call | solution.py:352
  101.6 0.0 copy-start
  101.6 0.7 copy-done
  102.3 0.6 copy.4
Async XLA Ops:
  101.6 0.7 copy-start

commit v3 on v2

--- a/solution.py
+++ b/solution.py
@@ -14,9 +14,17 @@
 D = NB * BLK
 N_DP = NC * NY * NZ
 PAIR = 4
-GATHER_AT = 2
+GATHER_AT = 1
 MESH = pl.DeviceIdType.MESH
 HIGH = lax.Precision.HIGHEST
+
+
+def split3(value):
+    high = value.astype(jnp.bfloat16)
+    rest = value - high.astype(jnp.float32)
+    mid = rest.astype(jnp.bfloat16)
+    low = (rest - mid.astype(jnp.float32)).astype(jnp.bfloat16)
+    return high, mid, low
 
 
 def lower_inverse(block):
@@ -57,32 +65,58 @@
             for r in range(q + 1, 8):
                 cols[r] = cols[r] - masked * mult[q][r]
         block[t] = own
-        for s in range(t + 1, groups):
-            cur = block[s]
-            coef = [jnp.broadcast_to(cur[:, base + q:base + q + 1], wide) for q in range(8)]
-            for q in range(8):
-                cur = jnp.where(lane == base + q, 0.0, cur) - coef[q] * rows[q]
-                for r in range(q + 1, 8):
-                    coef[r] = coef[r] - coef[q] * mult[q][r]
-            block[s] = cur
+        if t + 1 == groups:
+            continue
+        cur = block[t + 1]
+        coef = [jnp.broadcast_to(cur[:, base + q:base + q + 1], wide) for q in range(8)]
+        for q in range(8):
+            cur = jnp.where(lane == base + q, 0.0, cur) - coef[q] * rows[q]
+            for r in range(q + 1, 8):
+                coef[r] = coef[r] - coef[q] * mult[q][r]
+        block[t + 1] = cur
+        if t + 2 == groups:
+            continue
+        panel = (lane >= base) & (lane < base + 8)
+        rows = [jnp.where((lane > base + q) & (lane < base + 8), 0.0, rows[q]) for q in range(8)]
+        right = rows[0]
+        for q in range(1, 8):
+            right = jnp.where(sub == q, rows[q], right)
+        ah, am, al = split3(own)
+        bh, bm, bl = split3(right)
+        upd = lax.dot_general(jnp.concatenate([ah, ah, am, ah, al, am], axis=0),
+                              jnp.concatenate([bh, bm, bh, bl, bh, bm], axis=0),
+                              (((0,), (0,)), ((), ())), preferred_element_type=jnp.float32)
+        for s in range(t + 2, groups):
+            block[s] = jnp.where(panel, 0.0, block[s]) - upd[8 * s:8 * s + 8, :]
     for t in range(groups):
         diff = lane - sub - 8 * t
         block[t] = scales[t] * jnp.where(diff < 0, block[t], jnp.where(diff == 0, 1.0, 0.0))
     return block
 
 
-def tdot(a, b):
-    return lax.dot_general(a, b, (((0,), (0,)), ((), ())), precision=HIGH,
-                           preferred_element_type=jnp.float32)
+def stack_left(value, axis):
+    high, mid, low = split3(value)
+    return jnp.concatenate([high, high, mid, high, low, mid], axis=axis)
+
+
+def stack_right(value, axis):
+    high, mid, low = split3(value)
+    return jnp.concatenate([high, mid, high, low, high, mid], axis=axis)
+
+
+def mm(a, b):
+    return lax.dot_general(a, b, (((1,), (0,)), ((), ())), preferred_element_type=jnp.float32)
 
 
 def kernel(row_total, x_ref, ids_ref, out_ref,
            part, got_c, half, got_y, quarter, got_z, mom,
-           stage, send_rows, got, work, diag, white, rows, ret, ret_got,
+           stage, send_rows, between, got, work, diag, left, right, white, rows,
+           ret, ret_between, ret_got,
            c_send, c_recv, y_send, y_recv, z_send, z_recv,
            gz_send, gz_recv, a_send, a_recv, b_send, b_recv,
            a2_send, a2_recv, b2_send, b2_recv, gc_send, gc_recv,
-           d_send, d_recv, x_send, x_recv, r_send, r_recv):
+           d_send, d_recv, e_send, e_recv, x_send, x_recv,
+           r_send, r_recv, t_send, t_recv):
     f32, bf16 = jnp.float32, jnp.bfloat16
     m = lax.axis_index("mp")
     d = lax.axis_index("dp")
@@ -97,20 +131,18 @@
     y_peers = [lax.rem(y + o, NY) for o in (2, 1, 3)]
     z_peers = [lax.rem(z + o, NZ) for o in (8, 7, 9, 6, 10, 5, 11, 4, 12, 3, 13, 2, 14, 1, 15)]
     x_peers = [lax.rem(m + o, NX) for o in (2, 1, 3)]
+    plane = [(lax.rem(y + o, NY), co) for o in (2, 1, 3) for co in (1 - c, c)] + [(y, 1 - c)]
     barrier = pltpu.get_barrier_semaphore()
-
-    @pl.loop(1, N_DP)
-    def _(o):
-        pl.semaphore_signal(barrier, inc=1, device_id=(lax.rem(d + o, N_DP), m),
-                            device_id_type=MESH)
-    for p in x_peers:
-        pl.semaphore_signal(barrier, inc=1, device_id=(d, p), device_id_type=MESH)
+    everyone = ([dev(y, p, c, m) for p in z_peers] + [dev(yy, z, co, m) for yy, co in plane]
+                + [dev(y, z, c, p) for p in x_peers])
+    for peer in everyone:
+        pl.semaphore_signal(barrier, inc=1, device_id=peer, device_id_type=MESH)
 
     for i in range(NB):
         j = lax.rem(i + m, NB)
-        left = x_ref[:, i * BLK:(i + 1) * BLK]
-        right = x_ref[:, pl.ds(pl.multiple_of(j * BLK, BLK), BLK)]
-        prod = lax.dot_general(left, right, (((0,), (0,)), ((), ())),
+        lhs = x_ref[:, i * BLK:(i + 1) * BLK]
+        rhs = x_ref[:, pl.ds(pl.multiple_of(j * BLK, BLK), BLK)]
+        prod = lax.dot_general(lhs, rhs, (((0,), (0,)), ((), ())),
                                preferred_element_type=f32)
         part[:, :, :, i, :] = prod.reshape(NC, NY, NZ, BLK)
 
@@ -124,8 +156,7 @@
     earlier = (owner_row == owner_row.T) & (first < second)
     rank = jnp.sum(jnp.where(earlier, 1.0, 0.0), axis=0, keepdims=True)
     owner_iota = lax.broadcasted_iota(jnp.int32, (N_DP, count), 0).astype(f32)
-    own_hit = owner_iota == owner
-    pick = jnp.where(own_hit & (rank == m.astype(f32)), 1.0, 0.0)
+    pick = jnp.where((owner_iota == owner) & (rank == m.astype(f32)), 1.0, 0.0)
     picked = lax.dot_general(pick.astype(bf16), x_ref[...], (((1,), (0,)), ((), ())),
                              preferred_element_type=f32)
     label = jnp.sum(pick * within, axis=1, keepdims=True) - 1.0
@@ -133,9 +164,9 @@
         stage[:, i, :] = picked[:, i * BLK:(i + 1) * BLK]
     stage[:, NB, :] = jnp.broadcast_to(label, (N_DP, BLK))
     stage[:, NB + 1, :] = jnp.zeros((N_DP, BLK), f32)
-    send_rows[...] = stage[...].astype(bf16)
-    got[m, d] = send_rows[d]
-    pl.semaphore_wait(barrier, N_DP - 1 + NX - 1)
+    send_rows[...] = stage[...].astype(bf16).reshape(NY, NZ, NC, NB + 2, BLK)
+    between[y, c] = send_rows[y, :, c]
+    pl.semaphore_wait(barrier, len(everyone))
 
     def copy(src, dst, send, recv, device):
         return pltpu.make_async_remote_copy(
@@ -158,6 +189,11 @@
     quarter[...] = total
     for p in z_peers:
         cp = copy(quarter.at[p], got_z.at[z], z_send.at[p], z_recv.at[z], dev(y, p, c, m))
+        cp.start()
+        sent.append(cp)
+    for yy, co in plane:
+        cp = copy(send_rows.at[yy, :, co], between.at[y, c], d_send.at[yy * NC + co],
+                  d_recv.at[y * NC + c], dev(yy, z, co, m))
         cp.start()
         sent.append(cp)
     row = quarter[z]
@@ -171,13 +207,19 @@
         cp.start()
         sent.append(cp)
 
-    @pl.loop(1, N_DP)
-    def _(o):
-        p = lax.rem(d + o, N_DP)
-        copy(send_rows.at[p], got.at[m, d], d_send, d_recv, (p, m)).start()
     for p in reversed(z_peers):
         copy(mom.at[m, c, y, p], mom.at[m, c, y, p], gz_send.at[p], gz_recv.at[p],
              dev(y, p, c, m)).wait_recv()
+    for yy, co in plane:
+        copy(send_rows.at[yy, :, co], between.at[yy, co], d_send.at[yy * NC + co],
+             d_recv.at[yy * NC + co], dev(yy, z, co, m)).wait_recv()
+    late = []
+    for p in z_peers:
+        cp = copy(between.at[:, :, p], got.at[m, :, :, z], e_send.at[p], e_recv.at[z],
+                  dev(y, p, c, m))
+        cp.start()
+        late.append(cp)
+    got[m, :, :, z] = between[:, :, z]
     lo, hi = pl.ds(0, NZ // 2), pl.ds(NZ // 2, NZ // 2)
     for p in y_peers:
         cp = copy(mom.at[m, c, y, lo], mom.at[m, c, y, lo], a_send.at[p], a_recv.at[y],
@@ -219,6 +261,8 @@
         cp.wait_send()
     gc.wait_send()
 
+    for i in range(0, NB, 2):
+        white[i * BLK:(i + 1) * BLK, (i + 1) * BLK:(i + 2) * BLK] = jnp.zeros((BLK, BLK), bf16)
     scale = 1.0 / row_total
     eye = jnp.where(lax.broadcasted_iota(jnp.int32, (BLK, BLK), 0)
                     == lax.broadcasted_iota(jnp.int32, (BLK, BLK), 1), 0.001, 0.0)
@@ -245,8 +289,9 @@
             def _():
                 diag[...] = work[at(kk, kk)]
                 if kk == GATHER_AT:
-                    copy(send_rows.at[pl.ds(0, N_DP - 1)], got.at[m, pl.ds(0, N_DP - 1)],
-                         d_send, d_recv, sibling).wait()
+                    for p in z_peers:
+                        copy(between.at[:, :, p], got.at[m, :, :, p], e_send.at[p], e_recv.at[p],
+                             dev(y, p, c, m)).wait_recv()
                     for p in x_peers:
                         copy(got.at[m], got.at[m], x_send.at[p], x_recv.at[m],
                              (d, p)).start()
@@ -258,35 +303,40 @@
             def _():
                 rk = slice(kk * BLK, (kk + 1) * BLK)
                 inverse = diag[...]
-                line = lax.dot_general(inverse, work[rk, :], (((1,), (0,)), ((), ())),
-                                       precision=HIGH, preferred_element_type=f32)
-                work[rk, :] = line
-                work[at(kk, kk)] = inverse
-                for i in range(kk + 1, NB):
-                    ri = slice(i * BLK, (i + 1) * BLK)
-                    left = work[at(kk, i)]
-                    if kk:
-                        work[ri, :kk * BLK] = work[ri, :kk * BLK] - tdot(left, work[rk, :kk * BLK])
-                    work[at(i, kk)] = -tdot(left, inverse)
-                    work[ri, i * BLK:] = work[ri, i * BLK:] - tdot(left, work[rk, i * BLK:])
-
-    for k in range(NB):
-        for j in range(NB):
-            if j <= k:
-                white[at(k, j)] = work[at(k, j)].astype(bf16)
-            else:
-                white[at(k, j)] = jnp.zeros((BLK, BLK), bf16)
+                line = mm(stack_left(inverse, 1), stack_right(work[rk, :], 0))
+                white[at(kk, kk)] = inverse.astype(bf16)
+                if kk:
+                    white[rk, :kk * BLK] = line[:, :kk * BLK].astype(bf16)
+                if kk == NB - 1:
+                    return
+                done = (kk + 1) * BLK
+                left[done:, :] = stack_left(line[:, done:].T, 1)
+                right[:, :kk * BLK + BLK] = stack_right(
+                    jnp.concatenate([line[:, :kk * BLK], inverse], axis=1) if kk else inverse, 0)
+                right[:, done:] = stack_right(line[:, done:], 0)
+                old = mm(left[done:, :], right[:, :done])
+                if kk:
+                    work[done:, :kk * BLK] = work[done:, :kk * BLK] - old[:, :kk * BLK]
+                work[done:, rk] = -old[:, rk]
+                for i in range(kk + 1, NB, 2):
+                    ri = slice(i * BLK, min(i + 2, NB) * BLK)
+                    work[ri, i * BLK:] = work[ri, i * BLK:] - mm(left[ri, :], right[:, i * BLK:])
 
     for p in x_peers:
         copy(got.at[p], got.at[p], x_send.at[p], x_recv.at[p], (d, p)).wait()
+    for cp in late:
+        cp.wait_send()
     labels = []
     for k in range(PAIR):
-        stage[...] = got[k].astype(f32)
+        stage[...] = got[k].reshape(N_DP, NB + 2, BLK).astype(f32)
         for i in range(NB):
             rows[k * N_DP:(k + 1) * N_DP, i * BLK:(i + 1) * BLK] = stage[:, i, :].astype(bf16)
         labels.append(stage[:, NB, :])
-    whitened = lax.dot_general(rows[...], white[...], (((1,), (1,)), ((), ())),
-                               preferred_element_type=f32).astype(bf16)
+    wide = 2 * BLK
+    whitened = jnp.concatenate(
+        [lax.dot_general(rows[:, :n + wide], white[n:n + wide, :n + wide],
+                         (((1,), (1,)), ((), ())), preferred_element_type=f32)
+         for n in range(0, D, wide)], axis=1).astype(bf16)
     widened = whitened.astype(f32)
     square_sum = jnp.sum(widened * widened, axis=1, keepdims=True)
     rows[...] = (widened * lax.rsqrt(square_sum + 1e-06)).astype(bf16)
@@ -304,16 +354,32 @@
                 same = same & other
             best = jnp.maximum(best, jnp.where(same, sim[:, b * N_DP:(b + 1) * N_DP], -1.0))
         reply = jnp.where(lane == a, jnp.max(best, axis=1, keepdims=True), reply)
-    ret[:, 0, :] = reply
-    ret_got[d] = ret[d]
-
-    @pl.loop(1, N_DP)
-    def _(o):
-        p = lax.rem(d + o, N_DP)
-        copy(ret.at[p], ret_got.at[d], r_send, r_recv, (p, m)).start()
-    copy(ret.at[pl.ds(0, N_DP - 1)], ret_got.at[pl.ds(0, N_DP - 1)], r_send, r_recv,
-         sibling).wait()
-    table = lax.dot_general(ret_got[:, 0, :], jnp.where(own_hit, 1.0, 0.0),
+    ret[:, :, :, 0, :] = reply.reshape(NY, NC, NZ, BLK)
+    back = []
+    for p in z_peers:
+        cp = copy(ret.at[:, :, p], ret_between.at[z], r_send.at[p], r_recv.at[z], dev(y, p, c, m))
+        cp.start()
+        back.append(cp)
+    ret_between[z] = ret[:, :, z]
+    for p in reversed(z_peers):
+        copy(ret.at[:, :, p], ret_between.at[p], r_send.at[p], r_recv.at[p],
+             dev(y, p, c, m)).wait_recv()
+    for yy, co in plane:
+        cp = copy(ret_between.at[:, yy, co], ret_got.at[y, c], t_send.at[yy * NC + co],
+                  t_recv.at[y * NC + c], dev(yy, z, co, m))
+        cp.start()
+        back.append(cp)
+    ret_got[y, c] = ret_between[:, y, c]
+    spot = lax.broadcasted_iota(jnp.int32, (N_DP, count), 0)
+    spot_z, spot_yc = lax.rem(spot, NZ), lax.div(spot, NZ)
+    spot = (lax.div(spot_yc, NC) * NZ + spot_z) * NC + lax.rem(spot_yc, NC)
+    hit = jnp.where(spot.astype(f32) == owner, 1.0, 0.0)
+    for yy, co in plane:
+        copy(ret_between.at[:, yy, co], ret_got.at[yy, co], t_send.at[yy * NC + co],
+             t_recv.at[yy * NC + co], dev(yy, z, co, m)).wait_recv()
+    for cp in back:
+        cp.wait_send()
+    table = lax.dot_general(ret_got[:, :, :, 0, :].reshape(N_DP, BLK), hit,
                             (((0,), (0,)), ((), ())), precision=HIGH, preferred_element_type=f32)
     score = jnp.zeros((1, count), f32)
     for k in range(PAIR):
@@ -335,18 +401,23 @@
         pltpu.VMEM((NZ, NB, BLK), f32),
         pltpu.VMEM((NX, NC, NY, NZ, NB, BLK), f32),
         pltpu.VMEM((N_DP, NB + 2, BLK), f32),
-        pltpu.VMEM((N_DP, NB + 2, BLK), bf16),
-        pltpu.VMEM((NX, N_DP, NB + 2, BLK), bf16),
+        pltpu.VMEM((NY, NZ, NC, NB + 2, BLK), bf16),
+        pltpu.VMEM((NY, NC, NZ, NB + 2, BLK), bf16),
+        pltpu.VMEM((NX, NY, NC, NZ, NB + 2, BLK), bf16),
         pltpu.VMEM((D, D), f32),
         pltpu.VMEM((BLK, BLK), f32),
+        pltpu.VMEM((D, 6 * BLK), bf16),
+        pltpu.VMEM((6 * BLK, D), bf16),
         pltpu.VMEM((D, D), bf16),
         pltpu.VMEM((PAIR * N_DP, D), bf16),
-        pltpu.VMEM((N_DP, 1, BLK), f32),
-        pltpu.VMEM((N_DP, 1, BLK), f32),
+        pltpu.VMEM((NY, NC, NZ, 1, BLK), f32),
+        pltpu.VMEM((NZ, NY, NC, 1, BLK), f32),
+        pltpu.VMEM((NY, NC, NZ, 1, BLK), f32),
         dma, dma, dma((NY,)), dma((NY,)), dma((NZ,)), dma((NZ,)),
         dma((NZ,)), dma((NZ,)), dma((NY,)), dma((NY,)), dma((NX,)), dma((NX,)),
         dma((NX,)), dma((NX,)), dma((NY,)), dma((NY,)), dma, dma,
-        dma, dma, dma((NX,)), dma((NX,)), dma, dma,
+        dma((NY * NC,)), dma((NY * NC,)), dma((NZ,)), dma((NZ,)), dma((NX,)), dma((NX,)),
+        dma((NZ,)), dma((NZ,)), dma((NY * NC,)), dma((NY * NC,)),
     ]
     vm = pl.BlockSpec(memory_space=pltpu.VMEM)
     scores = pl.pallas_call(

time: 103 us -> 101 us (0.981)
  Pallas kernels: 102 us -> 99.2 us
    pallas_call x1, Pallas kernels: 102 us -> 99.2 us  [local(): pl.pallas_call(functools.partial(kernel, float(row_count * dp_count)), ou...]
where the time goes in v3:
time: 101 us; the launch traced here: 100 us
  Pallas kernels  99.2 us (98%)
  local copies, waits for them, and re-layouts  1.22 us (1%)
    pallas_call x1, Pallas kernels, local(): pl.pallas_call(functools.partial(kernel, float(row_count * dp_count)), ou...  99.2 us

profile of v3, /device:TPU:1, one launch (start us, length us, event | category | flops | bytes accessed | tf_op | source)
XLA Modules:
  0.0 100.5 jit_solution(10212353454400998199)
XLA Ops:
  0.0 99.2 %dedup.1 = f32[1,256]{1,0:T(1,128)} custom-call(bf16[256,768]{1,0:T(8,128)(2,1)} %x_ref.1, s32[1,256]{1,0:T(1,128)} %bitcast.3), custom_call_target="tpu_custom_call" | custom-call | tf_op jit(solution)/shard_map/dedup/pallas_call | solution.py:423
  99.2 0.0 copy-start
  99.3 0.7 copy-done
  99.9 0.6 copy.4
Async XLA Ops:
  99.2 0.7 copy-start

commit v4 on v3

--- a/solution.py
+++ b/solution.py
@@ -32,6 +32,7 @@
     sub = lax.broadcasted_iota(jnp.int32, (8, BLK), 0)
     groups = BLK // 8
     wide = (8, BLK)
+    picks = [jnp.full(wide, q, jnp.int32) for q in range(8)]
     scales = []
     for t in range(groups):
         own = block[t]
@@ -40,20 +41,28 @@
         piv = [[None] * 8 for _ in range(8)]
         for q in range(8):
             for r in range(q, 8):
-                piv[q][r] = jnp.broadcast_to(cols[r][q:q + 1, :], wide)
+                piv[q][r] = jnp.take_along_axis(cols[r], picks[q], axis=0)
         mult = [[None] * 8 for _ in range(8)]
         inv = [None] * 8
         scale = None
+        for q in range(0, 8, 2):
+            cross, last = piv[q][q + 1], piv[q + 1][q + 1]
+            minor = piv[q][q] * last - cross * cross
+            inv[q] = 1.0 / piv[q][q]
+            inv[q + 1] = piv[q][q] * (1.0 / minor)
+            mult[q][q + 1] = cross * inv[q]
+            piv[q + 1][q + 1] = minor * inv[q]
+            for r in range(q + 2, 8):
+                mult[q][r] = piv[q][r] * inv[q]
+                piv[q + 1][r] = piv[q + 1][r] - mult[q][q + 1] * piv[q][r]
+                mult[q + 1][r] = piv[q + 1][r] * inv[q + 1]
+            for r in range(q + 2, 8):
+                for s in range(r, 8):
+                    piv[r][s] = (piv[r][s] - mult[q][r] * piv[q][s]) - mult[q + 1][r] * piv[q + 1][s]
         for q in range(8):
-            inv[q] = 1.0 / piv[q][q]
-            for r in range(q + 1, 8):
-                mult[q][r] = piv[q][r] * inv[q]
-            for r in range(q + 1, 8):
-                for s in range(r, 8):
-                    piv[r][s] = piv[r][s] - mult[q][r] * piv[q][s]
-            root = lax.rsqrt(piv[q][q])
-            root = root * (1.5 - 0.5 * piv[q][q] * root * root)
-            scale = root if scale is None else jnp.where(sub == q, root, scale)
+            scale = piv[q][q] if scale is None else jnp.where(sub == q, piv[q][q], scale)
+        root = lax.rsqrt(scale)
+        scale = root * (1.5 - 0.5 * scale * root * root)
         scales.append(scale)
         rows = []
         for q in range(8):
@@ -109,7 +118,7 @@
 
 
 def kernel(row_total, x_ref, ids_ref, out_ref,
-           part, got_c, half, got_y, quarter, got_z, mom,
+           part, got_c, half, got_y, quarter, got_z, mom, flat,
            stage, send_rows, between, got, work, diag, left, right, white, rows,
            ret, ret_between, ret_got,
            c_send, c_recv, y_send, y_recv, z_send, z_recv,
@@ -161,10 +170,10 @@
                              preferred_element_type=f32)
     label = jnp.sum(pick * within, axis=1, keepdims=True) - 1.0
     for i in range(NB):
-        stage[:, i, :] = picked[:, i * BLK:(i + 1) * BLK]
-    stage[:, NB, :] = jnp.broadcast_to(label, (N_DP, BLK))
-    stage[:, NB + 1, :] = jnp.zeros((N_DP, BLK), f32)
-    send_rows[...] = stage[...].astype(bf16).reshape(NY, NZ, NC, NB + 2, BLK)
+        stage[pl.ds(i, N_DP, stride=NB + 2), :] = picked[:, i * BLK:(i + 1) * BLK]
+    stage[pl.ds(NB, N_DP, stride=NB + 2), :] = jnp.broadcast_to(label, (N_DP, BLK))
+    stage[pl.ds(NB + 1, N_DP, stride=NB + 2), :] = jnp.zeros((N_DP, BLK), f32)
+    send_rows[...] = stage[...].reshape(NY, NZ, NC, NB + 2, BLK).astype(bf16)
     between[y, c] = send_rows[y, :, c]
     pl.semaphore_wait(barrier, len(everyone))
 
@@ -221,6 +230,21 @@
         late.append(cp)
     got[m, :, :, z] = between[:, :, z]
     lo, hi = pl.ds(0, NZ // 2), pl.ds(NZ // 2, NZ // 2)
+
+    def piece(n, core):
+        kind, peer = divmod(n + 2, 3)
+        return (mom.at[m, core, y],
+                mom.at[m, core, y_peers[peer], lo],
+                mom.at[x_peers[peer], core, y, hi],
+                mom.at[x_peers[peer], core, :, lo],
+                mom.at[:, core, y_peers[peer], hi])[kind]
+
+    def pass_on(n):
+        cp = copy(piece(n, c), piece(n, c), gc_send.at[n], gc_recv.at[n], sibling)
+        cp.start()
+        sent.append(cp)
+
+    pass_on(0)
     for p in y_peers:
         cp = copy(mom.at[m, c, y, lo], mom.at[m, c, y, lo], a_send.at[p], a_recv.at[y],
                   dev(p, z, c, m))
@@ -231,35 +255,37 @@
                   dev(y, z, c, p))
         cp.start()
         sent.append(cp)
-    for p in y_peers:
+    for n, p in enumerate(y_peers):
         copy(mom.at[m, c, p, lo], mom.at[m, c, p, lo], a_send.at[p], a_recv.at[p],
              dev(p, z, c, m)).wait_recv()
+        pass_on(1 + n)
     for p in x_peers:
         cp = copy(mom.at[m, c, :, lo], mom.at[m, c, :, lo], a2_send.at[p], a2_recv.at[m],
                   dev(y, z, c, p))
         cp.start()
         sent.append(cp)
-    for p in x_peers:
+    for n, p in enumerate(x_peers):
         copy(mom.at[p, c, y, hi], mom.at[p, c, y, hi], b_send.at[p], b_recv.at[p],
              dev(y, z, c, p)).wait_recv()
+        pass_on(4 + n)
     for p in y_peers:
         cp = copy(mom.at[:, c, y, hi], mom.at[:, c, y, hi], b2_send.at[p], b2_recv.at[y],
                   dev(p, z, c, m))
         cp.start()
         sent.append(cp)
-    for p in x_peers:
+    for n, p in enumerate(x_peers):
         copy(mom.at[p, c, :, lo], mom.at[p, c, :, lo], a2_send.at[p], a2_recv.at[p],
              dev(y, z, c, p)).wait_recv()
-    for p in y_peers:
+        pass_on(7 + n)
+    for n, p in enumerate(y_peers):
         copy(mom.at[:, c, p, hi], mom.at[:, c, p, hi], b2_send.at[p], b2_recv.at[p],
              dev(p, z, c, m)).wait_recv()
-    gc = copy(mom.at[:, c], mom.at[:, c], gc_send, gc_recv, sibling)
-    gc.start()
-    copy(mom.at[:, 1 - c], mom.at[:, 1 - c], gc_send, gc_recv, sibling).wait_recv()
+        pass_on(10 + n)
+    for n in range(13):
+        copy(piece(n, 1 - c), piece(n, 1 - c), gc_send.at[n], gc_recv.at[n], sibling).wait_recv()
     cc.wait_send()
     for cp in sent:
         cp.wait_send()
-    gc.wait_send()
 
     for i in range(0, NB, 2):
         white[i * BLK:(i + 1) * BLK, (i + 1) * BLK:(i + 2) * BLK] = jnp.zeros((BLK, BLK), bf16)
@@ -271,7 +297,13 @@
         return (slice(i * BLK, (i + 1) * BLK), slice(j * BLK, (j + 1) * BLK))
 
     def moment_block(g, i):
-        return mom[g, :, :, :, i, :].reshape(BLK, BLK) * scale
+        return flat[pl.ds(g * N_DP * 8 + i, N_DP, stride=8), :] * scale
+
+    @pl.loop(0, NX * N_DP // 16)
+    def _(b):
+        for r in range(16):
+            flat[pl.ds(pl.multiple_of(b * BLK, BLK) + 8 * r, NB), :] = (
+                mom[lax.div(b, 8), lax.div(lax.rem(b, 8), 4), lax.rem(b, 4), r])
 
     for i in range(NB):
         for g in range(4):
@@ -328,10 +360,11 @@
         cp.wait_send()
     labels = []
     for k in range(PAIR):
-        stage[...] = got[k].reshape(N_DP, NB + 2, BLK).astype(f32)
+        stage[...] = got[k].astype(f32).reshape(N_DP * (NB + 2), BLK)
         for i in range(NB):
-            rows[k * N_DP:(k + 1) * N_DP, i * BLK:(i + 1) * BLK] = stage[:, i, :].astype(bf16)
-        labels.append(stage[:, NB, :])
+            rows[k * N_DP:(k + 1) * N_DP, i * BLK:(i + 1) * BLK] = (
+                stage[pl.ds(i, N_DP, stride=NB + 2), :].astype(bf16))
+        labels.append(stage[pl.ds(NB, N_DP, stride=NB + 2), :])
     wide = 2 * BLK
     whitened = jnp.concatenate(
         [lax.dot_general(rows[:, :n + wide], white[n:n + wide, :n + wide],
@@ -400,7 +433,8 @@
         pltpu.VMEM((NZ, NB, BLK), f32),
         pltpu.VMEM((NZ, NB, BLK), f32),
         pltpu.VMEM((NX, NC, NY, NZ, NB, BLK), f32),
-        pltpu.VMEM((N_DP, NB + 2, BLK), f32),
+        pltpu.VMEM((NX * N_DP * 8, BLK), f32),
+        pltpu.VMEM((N_DP * (NB + 2), BLK), f32),
         pltpu.VMEM((NY, NZ, NC, NB + 2, BLK), bf16),
         pltpu.VMEM((NY, NC, NZ, NB + 2, BLK), bf16),
         pltpu.VMEM((NX, NY, NC, NZ, NB + 2, BLK), bf16),
@@ -415,7 +449,7 @@
         pltpu.VMEM((NY, NC, NZ, 1, BLK), f32),
         dma, dma, dma((NY,)), dma((NY,)), dma((NZ,)), dma((NZ,)),
         dma((NZ,)), dma((NZ,)), dma((NY,)), dma((NY,)), dma((NX,)), dma((NX,)),
-        dma((NX,)), dma((NX,)), dma((NY,)), dma((NY,)), dma, dma,
+        dma((NX,)), dma((NX,)), dma((NY,)), dma((NY,)), dma((13,)), dma((13,)),
         dma((NY * NC,)), dma((NY * NC,)), dma((NZ,)), dma((NZ,)), dma((NX,)), dma((NX,)),
         dma((NZ,)), dma((NZ,)), dma((NY * NC,)), dma((NY * NC,)),
     ]

time: 101 us -> 93.2 us (0.923)
  Pallas kernels: 99.2 us -> 91.8 us
    pallas_call x1, Pallas kernels: 99.2 us -> 91.8 us  [local(): pl.pallas_call(functools.partial(kernel, float(row_count * dp_count)), ou...]
where the time goes in v4:
time: 93.2 us; the launch traced here: 93 us
  Pallas kernels  91.8 us (98%)
  local copies, waits for them, and re-layouts  1.22 us (1%)
    pallas_call x1, Pallas kernels, local(): pl.pallas_call(functools.partial(kernel, float(row_count * dp_count)), ou...  91.8 us

profile of v4, /device:TPU:1, one launch (start us, length us, event | category | flops | bytes accessed | tf_op | source)
XLA Modules:
  0.0 93.0 jit_solution(13667873182141684363)
XLA Ops:
  0.0 91.8 %dedup.1 = f32[1,256]{1,0:T(1,128)} custom-call(bf16[256,768]{1,0:T(8,128)(2,1)} %x_ref.1, s32[1,256]{1,0:T(1,128)} %bitcast.3), custom_call_target="tpu_custom_call" | custom-call | tf_op jit(solution)/shard_map/dedup/pallas_call | solution.py:457
  91.8 0.0 copy-start
  91.8 0.7 copy-done
  92.5 0.6 copy.4
Async XLA Ops:
  91.8 0.7 copy-start

commit v5 on v4

--- a/solution.py
+++ b/solution.py
@@ -15,6 +15,7 @@
 N_DP = NC * NY * NZ
 PAIR = 4
 GATHER_AT = 1
+RELAY_AT = 3
 MESH = pl.DeviceIdType.MESH
 HIGH = lax.Precision.HIGHEST
 
@@ -119,12 +120,12 @@
 
 def kernel(row_total, x_ref, ids_ref, out_ref,
            part, got_c, half, got_y, quarter, got_z, mom, flat,
-           stage, send_rows, between, got, work, diag, left, right, white, rows,
+           stage, send_rows, between, got, work, left, right, white, rows,
            ret, ret_between, ret_got,
            c_send, c_recv, y_send, y_recv, z_send, z_recv,
            gz_send, gz_recv, a_send, a_recv, b_send, b_recv,
            a2_send, a2_recv, b2_send, b2_recv, gc_send, gc_recv,
-           d_send, d_recv, e_send, e_recv, x_send, x_recv,
+           d_send, d_recv, e_send, e_recv, x_send, x_recv, f_send, f_recv,
            r_send, r_recv, t_send, t_recv):
     f32, bf16 = jnp.float32, jnp.bfloat16
     m = lax.axis_index("mp")
@@ -314,57 +315,63 @@
             elif g < 3:
                 work[at(j - NB, i)] = moment_block(g, i).T
 
-    @pl.loop(0, NB)
-    def _(k):
-        for kk in range(NB):
-            @pl.when(k == kk)
-            def _():
-                diag[...] = work[at(kk, kk)]
-                if kk == GATHER_AT:
-                    for p in z_peers:
-                        copy(between.at[:, :, p], got.at[m, :, :, p], e_send.at[p], e_recv.at[p],
-                             dev(y, p, c, m)).wait_recv()
-                    for p in x_peers:
-                        copy(got.at[m], got.at[m], x_send.at[p], x_recv.at[m],
-                             (d, p)).start()
-        block = lower_inverse([diag[8 * t:8 * t + 8, :] for t in range(BLK // 8)])
-        for t in range(BLK // 8):
-            diag[8 * t:8 * t + 8, :] = block[t]
-        for kk in range(NB):
-            @pl.when(k == kk)
-            def _():
-                rk = slice(kk * BLK, (kk + 1) * BLK)
-                inverse = diag[...]
-                line = mm(stack_left(inverse, 1), stack_right(work[rk, :], 0))
-                white[at(kk, kk)] = inverse.astype(bf16)
-                if kk:
-                    white[rk, :kk * BLK] = line[:, :kk * BLK].astype(bf16)
-                if kk == NB - 1:
-                    return
-                done = (kk + 1) * BLK
-                left[done:, :] = stack_left(line[:, done:].T, 1)
-                right[:, :kk * BLK + BLK] = stack_right(
-                    jnp.concatenate([line[:, :kk * BLK], inverse], axis=1) if kk else inverse, 0)
-                right[:, done:] = stack_right(line[:, done:], 0)
-                old = mm(left[done:, :], right[:, :done])
-                if kk:
-                    work[done:, :kk * BLK] = work[done:, :kk * BLK] - old[:, :kk * BLK]
-                work[done:, rk] = -old[:, rk]
-                for i in range(kk + 1, NB, 2):
-                    ri = slice(i * BLK, min(i + 2, NB) * BLK)
-                    work[ri, i * BLK:] = work[ri, i * BLK:] - mm(left[ri, :], right[:, i * BLK:])
-
-    for p in x_peers:
-        copy(got.at[p], got.at[p], x_send.at[p], x_recv.at[p], (d, p)).wait()
+    labels = []
+    following, previous, opposite = (lax.rem(m + o, NX) for o in (1, 3, 2))
+    halves = (pl.ds(0, NY // 2), pl.ds(NY // 2, NY // 2))
+    corner = work[at(0, 0)]
+    for kk in range(NB):
+        if kk == GATHER_AT:
+            for p in z_peers:
+                copy(between.at[:, :, p], got.at[m, :, :, p], e_send.at[p], e_recv.at[p],
+                     dev(y, p, c, m)).wait_recv()
+            for p in (following, previous):
+                cp = copy(got.at[m], got.at[m], x_send.at[p], x_recv.at[m], (d, p))
+                cp.start()
+                late.append(cp)
+        if kk == RELAY_AT:
+            for p in (following, previous):
+                copy(got.at[p], got.at[p], x_send.at[p], x_recv.at[p], (d, p)).wait_recv()
+            for n, (source, p) in enumerate(((previous, following), (following, previous))):
+                part_of = got.at[source, halves[n]]
+                cp = copy(part_of, part_of, f_send.at[n], f_recv.at[n], (d, p))
+                cp.start()
+                late.append(cp)
+        if kk == NB - 1:
+            for n, p in enumerate((previous, following)):
+                part_of = got.at[opposite, halves[n]]
+                copy(part_of, part_of, f_send.at[n], f_recv.at[n], (d, p)).wait_recv()
+            for k in range(PAIR):
+                stage[...] = got[k].astype(f32).reshape(N_DP * (NB + 2), BLK)
+                for i in range(NB):
+                    rows[k * N_DP:(k + 1) * N_DP, i * BLK:(i + 1) * BLK] = (
+                        stage[pl.ds(i, N_DP, stride=NB + 2), :].astype(bf16))
+                labels.append(stage[pl.ds(NB, N_DP, stride=NB + 2), :])
+        inverse = jnp.concatenate(
+            lower_inverse([corner[8 * t:8 * t + 8, :] for t in range(BLK // 8)]), axis=0)
+        rk = slice(kk * BLK, (kk + 1) * BLK)
+        line = mm(stack_left(inverse, 1), stack_right(work[rk, :], 0))
+        white[at(kk, kk)] = inverse.astype(bf16)
+        if kk:
+            white[rk, :kk * BLK] = line[:, :kk * BLK].astype(bf16)
+        if kk == NB - 1:
+            break
+        done = (kk + 1) * BLK
+        left[done:, :] = stack_left(line[:, done:].T, 1)
+        right[:, done:] = stack_right(line[:, done:], 0)
+        nxt = at(kk + 1, kk + 1)
+        corner = work[nxt] - mm(left[nxt[0], :], right[:, nxt[1]])
+        right[:, :done] = stack_right(
+            jnp.concatenate([line[:, :kk * BLK], inverse], axis=1) if kk else inverse, 0)
+        old = mm(left[done:, :], right[:, :done])
+        if kk:
+            work[done:, :kk * BLK] = work[done:, :kk * BLK] - old[:, :kk * BLK]
+        work[done:, rk] = -old[:, rk]
+        for i in range(kk + 1, NB, 2):
+            ri = slice(i * BLK, min(i + 2, NB) * BLK)
+            work[ri, i * BLK:] = work[ri, i * BLK:] - mm(left[ri, :], right[:, i * BLK:])
+
     for cp in late:
         cp.wait_send()
-    labels = []
-    for k in range(PAIR):
-        stage[...] = got[k].astype(f32).reshape(N_DP * (NB + 2), BLK)
-        for i in range(NB):
-            rows[k * N_DP:(k + 1) * N_DP, i * BLK:(i + 1) * BLK] = (
-                stage[pl.ds(i, N_DP, stride=NB + 2), :].astype(bf16))
-        labels.append(stage[pl.ds(NB, N_DP, stride=NB + 2), :])
     wide = 2 * BLK
     whitened = jnp.concatenate(
         [lax.dot_general(rows[:, :n + wide], white[n:n + wide, :n + wide],
@@ -439,7 +446,6 @@
         pltpu.VMEM((NY, NC, NZ, NB + 2, BLK), bf16),
         pltpu.VMEM((NX, NY, NC, NZ, NB + 2, BLK), bf16),
         pltpu.VMEM((D, D), f32),
-        pltpu.VMEM((BLK, BLK), f32),
         pltpu.VMEM((D, 6 * BLK), bf16),
         pltpu.VMEM((6 * BLK, D), bf16),
         pltpu.VMEM((D, D), bf16),
@@ -450,7 +456,7 @@
         dma, dma, dma((NY,)), dma((NY,)), dma((NZ,)), dma((NZ,)),
         dma((NZ,)), dma((NZ,)), dma((NY,)), dma((NY,)), dma((NX,)), dma((NX,)),
         dma((NX,)), dma((NX,)), dma((NY,)), dma((NY,)), dma((13,)), dma((13,)),
-        dma((NY * NC,)), dma((NY * NC,)), dma((NZ,)), dma((NZ,)), dma((NX,)), dma((NX,)),
+        dma((NY * NC,)), dma((NY * NC,)), dma((NZ,)), dma((NZ,)), dma((NX,)), dma((NX,)), dma((2,)), dma((2,)),
         dma((NZ,)), dma((NZ,)), dma((NY * NC,)), dma((NY * NC,)),
     ]
     vm = pl.BlockSpec(memory_space=pltpu.VMEM)

time: 93.2 us -> 92.3 us (level)
  no operation moved by 1% of the time
where the time goes in v5:
time: 92.3 us; the launch traced here: 92.2 us
  Pallas kernels  90.9 us (98%)
  local copies, waits for them, and re-layouts  1.22 us (1%)
    pallas_call x1, Pallas kernels, local(): pl.pallas_call(functools.partial(kernel, float(row_count * dp_count)), ou...  90.9 us

profile of v5, /device:TPU:1, one launch (start us, length us, event | category | flops | bytes accessed | tf_op | source)
XLA Modules:
  0.0 92.2 jit_solution(14495437164837463305)
XLA Ops:
  0.0 90.9 %dedup.1 = f32[1,256]{1,0:T(1,128)} custom-call(bf16[256,768]{1,0:T(8,128)(2,1)} %x_ref.1, s32[1,256]{1,0:T(1,128)} %bitcast.3), custom_call_target="tpu_custom_call" | custom-call | tf_op jit(solution)/shard_map/dedup/pallas_call | solution.py:463
  90.9 0.0 copy-start
  91.0 0.7 copy-done
  91.6 0.6 copy.4
Async XLA Ops:
  90.9 0.7 copy-start

commit v6 on v5

--- a/solution.py
+++ b/solution.py
@@ -183,15 +183,19 @@
             src_ref=src, dst_ref=dst, send_sem=send, recv_sem=recv,
             device_id=device, device_id_type=MESH)
 
-    cc = copy(part.at[1 - c], got_c, c_send, c_recv, sibling)
-    cc.start()
-    cc.wait_recv()
-    half[...] = part[c] + got_c[...]
     sent = []
-    for p in y_peers:
-        cp = copy(half.at[p], got_y.at[y], y_send.at[p], y_recv.at[y], dev(p, z, c, m))
-        cp.start()
-        sent.append(cp)
+    order = y_peers + [y]
+    for p in order:
+        cp = copy(part.at[1 - c, p], got_c.at[p], c_send.at[p], c_recv.at[p], sibling)
+        cp.start()
+        sent.append(cp)
+    for p in order:
+        copy(part.at[1 - c, p], got_c.at[p], c_send.at[p], c_recv.at[p], sibling).wait_recv()
+        half[p] = part[c, p] + got_c[p]
+        if p is not y:
+            cp = copy(half.at[p], got_y.at[y], y_send.at[p], y_recv.at[y], dev(p, z, c, m))
+            cp.start()
+            sent.append(cp)
     total = half[y]
     for p in y_peers:
         copy(half.at[p], got_y.at[p], y_send.at[p], y_recv.at[p], dev(p, z, c, m)).wait_recv()
@@ -245,7 +249,6 @@
         cp.start()
         sent.append(cp)
 
-    pass_on(0)
     for p in y_peers:
         cp = copy(mom.at[m, c, y, lo], mom.at[m, c, y, lo], a_send.at[p], a_recv.at[y],
                   dev(p, z, c, m))
@@ -256,35 +259,48 @@
                   dev(y, z, c, p))
         cp.start()
         sent.append(cp)
-    for n, p in enumerate(y_peers):
+
+    def low_piece(q):
+        for p in x_peers:
+            cp = copy(mom.at[m, c, q, lo], mom.at[m, c, q, lo], a2_send.at[p * NY + q],
+                      a2_recv.at[m * NY + q], dev(y, z, c, p))
+            cp.start()
+            sent.append(cp)
+
+    def high_piece(q):
+        for p in y_peers:
+            cp = copy(mom.at[q, c, y, hi], mom.at[q, c, y, hi], b2_send.at[p * NX + q],
+                      b2_recv.at[y * NX + q], dev(p, z, c, m))
+            cp.start()
+            sent.append(cp)
+
+    low_piece(y)
+    high_piece(m)
+    pass_on(0)
+    for n in (1, 2, 0):
+        p = y_peers[n]
         copy(mom.at[m, c, p, lo], mom.at[m, c, p, lo], a_send.at[p], a_recv.at[p],
              dev(p, z, c, m)).wait_recv()
+        low_piece(p)
         pass_on(1 + n)
-    for p in x_peers:
-        cp = copy(mom.at[m, c, :, lo], mom.at[m, c, :, lo], a2_send.at[p], a2_recv.at[m],
-                  dev(y, z, c, p))
-        cp.start()
-        sent.append(cp)
-    for n, p in enumerate(x_peers):
+        p = x_peers[n]
         copy(mom.at[p, c, y, hi], mom.at[p, c, y, hi], b_send.at[p], b_recv.at[p],
              dev(y, z, c, p)).wait_recv()
+        high_piece(p)
         pass_on(4 + n)
-    for p in y_peers:
-        cp = copy(mom.at[:, c, y, hi], mom.at[:, c, y, hi], b2_send.at[p], b2_recv.at[y],
-                  dev(p, z, c, m))
-        cp.start()
-        sent.append(cp)
-    for n, p in enumerate(x_peers):
-        copy(mom.at[p, c, :, lo], mom.at[p, c, :, lo], a2_send.at[p], a2_recv.at[p],
-             dev(y, z, c, p)).wait_recv()
+    for n in (1, 2, 0):
+        p = x_peers[n]
+        for q in range(NY):
+            copy(mom.at[p, c, q, lo], mom.at[p, c, q, lo], a2_send.at[p * NY + q],
+                 a2_recv.at[p * NY + q], dev(y, z, c, p)).wait_recv()
         pass_on(7 + n)
-    for n, p in enumerate(y_peers):
-        copy(mom.at[:, c, p, hi], mom.at[:, c, p, hi], b2_send.at[p], b2_recv.at[p],
-             dev(p, z, c, m)).wait_recv()
+        p = y_peers[n]
+        for q in range(NX):
+            copy(mom.at[q, c, p, hi], mom.at[q, c, p, hi], b2_send.at[p * NX + q],
+                 b2_recv.at[p * NX + q], dev(p, z, c, m)).wait_recv()
         pass_on(10 + n)
     for n in range(13):
         copy(piece(n, 1 - c), piece(n, 1 - c), gc_send.at[n], gc_recv.at[n], sibling).wait_recv()
-    cc.wait_send()
     for cp in sent:
         cp.wait_send()
 
@@ -453,9 +469,10 @@
         pltpu.VMEM((NY, NC, NZ, 1, BLK), f32),
         pltpu.VMEM((NZ, NY, NC, 1, BLK), f32),
         pltpu.VMEM((NY, NC, NZ, 1, BLK), f32),
-        dma, dma, dma((NY,)), dma((NY,)), dma((NZ,)), dma((NZ,)),
+        dma((NY,)), dma((NY,)), dma((NY,)), dma((NY,)), dma((NZ,)), dma((NZ,)),
         dma((NZ,)), dma((NZ,)), dma((NY,)), dma((NY,)), dma((NX,)), dma((NX,)),
-        dma((NX,)), dma((NX,)), dma((NY,)), dma((NY,)), dma((13,)), dma((13,)),
+        dma((NX * NY,)), dma((NX * NY,)), dma((NX * NY,)), dma((NX * NY,)),
+        dma((13,)), dma((13,)),
         dma((NY * NC,)), dma((NY * NC,)), dma((NZ,)), dma((NZ,)), dma((NX,)), dma((NX,)), dma((2,)), dma((2,)),
         dma((NZ,)), dma((NZ,)), dma((NY * NC,)), dma((NY * NC,)),
     ]

time: 92.3 us -> 91.4 us (level)
    pallas_call x1, Pallas kernels: 90.9 us -> 90 us  [local(): pl.pallas_call(functools.partial(kernel, float(row_count * dp_count)), ou...]
where the time goes in v6:
time: 91.4 us; the launch traced here: 91.2 us
  Pallas kernels  90 us (98%)
  local copies, waits for them, and re-layouts  1.22 us (1%)
    pallas_call x1, Pallas kernels, local(): pl.pallas_call(functools.partial(kernel, float(row_count * dp_count)), ou...  90 us

profile of v6, /device:TPU:1, one launch (start us, length us, event | category | flops | bytes accessed | tf_op | source)
XLA Modules:
  0.0 91.2 jit_solution(13622896500600946263)
XLA Ops:
  0.0 90.0 %dedup.1 = f32[1,256]{1,0:T(1,128)} custom-call(bf16[256,768]{1,0:T(8,128)(2,1)} %x_ref.1, s32[1,256]{1,0:T(1,128)} %bitcast.3), custom_call_target="tpu_custom_call" | custom-call | tf_op jit(solution)/shard_map/dedup/pallas_call | solution.py:480
  90.0 0.0 copy-start
  90.0 0.7 copy-done
  90.6 0.6 copy.4
Async XLA Ops:
  90.0 0.7 copy-start

commit v7 on v6

--- a/solution.py
+++ b/solution.py
@@ -205,11 +205,6 @@
         cp = copy(quarter.at[p], got_z.at[z], z_send.at[p], z_recv.at[z], dev(y, p, c, m))
         cp.start()
         sent.append(cp)
-    for yy, co in plane:
-        cp = copy(send_rows.at[yy, :, co], between.at[y, c], d_send.at[yy * NC + co],
-                  d_recv.at[y * NC + c], dev(yy, z, co, m))
-        cp.start()
-        sent.append(cp)
     row = quarter[z]
     for p in reversed(z_peers):
         copy(quarter.at[p], got_z.at[p], z_send.at[p], z_recv.at[p], dev(y, p, c, m)).wait_recv()
@@ -221,6 +216,11 @@
         cp.start()
         sent.append(cp)
 
+    for yy, co in plane:
+        cp = copy(send_rows.at[yy, :, co], between.at[y, c], d_send.at[yy * NC + co],
+                  d_recv.at[y * NC + c], dev(yy, z, co, m))
+        cp.start()
+        sent.append(cp)
     for p in reversed(z_peers):
         copy(mom.at[m, c, y, p], mom.at[m, c, y, p], gz_send.at[p], gz_recv.at[p],
              dev(y, p, c, m)).wait_recv()

time: 91.4 us -> 91.4 us (level)
  no operation moved by 1% of the time
where the time goes in v7:
time: 91.4 us; the launch traced here: 91.2 us
  Pallas kernels  90 us (98%)
  local copies, waits for them, and re-layouts  1.22 us (1%)
    pallas_call x1, Pallas kernels, local(): pl.pallas_call(functools.partial(kernel, float(row_count * dp_count)), ou...  90 us

profile of v7, /device:TPU:1, one launch (start us, length us, event | category | flops | bytes accessed | tf_op | source)
XLA Modules:
  0.0 91.2 jit_solution(8574232482622242756)
XLA Ops:
  0.0 90.0 %dedup.1 = f32[1,256]{1,0:T(1,128)} custom-call(bf16[256,768]{1,0:T(8,128)(2,1)} %x_ref.1, s32[1,256]{1,0:T(1,128)} %bitcast.3), custom_call_target="tpu_custom_call" | custom-call | tf_op jit(solution)/shard_map/dedup/pallas_call | solution.py:480
  90.0 0.0 copy-start
  90.0 0.7 copy-done
  90.6 0.6 copy.4
Async XLA Ops:
  90.0 0.7 copy-start
